TPU v7x, 32 devices: a whole 2x2x4 slice. The times are simulated.
32 devices in a mesh: wave: 8 (over z, y), lev: 4 (over x, core).
Axes of the slice: x: 2, y: 2, z: 4, core: 2. Of those that a mesh axis runs over, the one named last changes fastest.
Arguments:
- fine_state: float32 [8, 3, 2, 24, 49], P('lev', None, None, 'wave'), may hold values from -6 to 6
- fold_pairs: int32 [24], replicated, may hold values from 0 to 23, each once
- legendre: bfloat16 [24, 96, 49], P('wave', 'lev'), may hold values from -0.875 to 0.875
- gauss_weights: float32 [96], P('lev'), may hold values from 0.5 to 3
- grid_coef: float32 [8, 2560], replicated, may hold values from -4 to 4
- modes_from: float32 [8, 8], replicated
- modes_to: float32 [8, 8], replicated, as said below
- mode_rates: float32 [8], replicated, may hold values from 0.2 to 20
Outputs:
- corrected: float32 [8, 2, 2, 24, 49], P('lev', None, None, 'wave')
- fine_tend: float32 [8, 3, 2, 24, 49], P('lev', None, None, 'wave')
Inputs may be any that keep to these rules, and one draw needn't show every extreme that they name: Slot p holds zonal wavenumbers fold_pairs[p] and 47 - fold_pairs[p]; every value occurs once. modes_to is the inverse of modes_from.
All inputs are finite; a program needn't handle non-finite values.
Results may differ from a plain program's by a relative error of at most 0.02.
Values may be sent and summed in bfloat16 or wider, within the bound.
No kernel may reach another device: no remote copies, remote signals or barrier semaphores. Data moves between devices by JAX's collectives and lax.ppermute only.
A program may use at most 64 MiB of HBM per device.

v0:
```python
import functools
import math

import jax
import jax.numpy as jnp
import numpy as np
from jax import lax
from jax.experimental import pallas as pl
from jax.experimental.pallas import tpu as pltpu
from jax.sharding import PartitionSpec as P

STEP_HALF = 0.5
quad_weights = ((5.0 / 24.0, 1.0 / 3.0, -1.0 / 24.0), (-1.0 / 24.0, 1.0 / 3.0, 5.0 / 24.0))
HIGHEST = lax.Precision.HIGHEST


def fourier_table(waves, points, amplitude):
    steps = jnp.arange(points, dtype=jnp.int32)
    turns = waves[:, :, None] * steps[None, None, :] % points
    angles = turns.astype(jnp.float32) * (2.0 * math.pi / points)
    return jnp.stack([jnp.cos(angles) * amplitude, -jnp.sin(angles) * amplitude]).astype(
        jnp.bfloat16
    )


def fine_rows(small_wave, fine_width):
    row_ids = jnp.arange(fine_width + 1, dtype=jnp.int32)[None, :]
    return row_ids < fine_width - small_wave[:, None]


def coarse_rows(small_wave, coarse):
    row_ids = jnp.arange(coarse, dtype=jnp.int32)[None, :]
    coarse_keep = row_ids < coarse - small_wave[:, None]
    degree = (small_wave[:, None] + row_ids).astype(jnp.float32)
    return (coarse_keep, degree)


def legendre_inverse(spectral, legendre_table, row_mask):
    split_spec = spectral[:, :, :, :, None, :] * row_mask[None, None, None]
    return jnp.einsum(
        "abcpmr,plr->abcpml", split_spec, legendre_table, preferred_element_type=jnp.float32
    ).astype(jnp.bfloat16)


def legendre_forward(returned, legendre_table, row_mask):
    members = jnp.einsum(
        "abcpml,plr->abcpmr", returned, legendre_table, preferred_element_type=jnp.float32
    )
    return jnp.sum(members * row_mask.astype(jnp.float32)[None, None, None], axis=4)


def grid_step(fourier, wave_table, coef, weights, factor):
    grid_field = jnp.einsum(
        "abcpmz,cpmk->abzk", fourier, wave_table, preferred_element_type=jnp.float32
    )
    product = (coef[:, None, None, :] * grid_field * grid_field).astype(jnp.bfloat16)
    returned = jnp.einsum(
        "abzk,cpmk->abcpmz", product, wave_table, preferred_element_type=jnp.float32
    )
    return (returned * (weights * factor)).astype(jnp.bfloat16)


def mix(matrix, values):
    return jnp.einsum("ql,lbcpr->qbcpr", matrix, values, precision=HIGHEST)


def split_plan(
    fine_state, fold_pairs, legendre, gauss_weights, grid_coef, modes_from, modes_to, mode_rates
):
    n_wave = lax.axis_size("wave")
    wave_idx = lax.axis_index("wave")
    lev_idx = lax.axis_index("lev")
    lev_dev = fine_state.shape[0]
    pairs_dev = fine_state.shape[3]
    fine_width = fine_state.shape[4] - 1
    coarse = fine_width // 2
    longitudes = grid_coef.shape[1]
    band_size = legendre.shape[1] // n_wave
    small_wave = lax.dynamic_slice_in_dim(fold_pairs, wave_idx * pairs_dev, pairs_dev)
    first_member = fine_rows(small_wave, fine_width)
    member_mask = jnp.stack([first_member, jnp.logical_not(first_member)], 1).astype(jnp.bfloat16)
    coarse_keep, degree = coarse_rows(small_wave, coarse)
    keep_mask = coarse_keep[:, None, :].astype(jnp.bfloat16)
    keep_float = coarse_keep.astype(jnp.float32)
    fine_table = fourier_table(
        jnp.stack([fold_pairs, fine_width - 1 - fold_pairs], 1), longitudes, fine_width ** (-0.5)
    )
    coarse_table = fourier_table(fold_pairs[:, None], longitudes // 2, coarse ** (-0.5))
    coarse_leg = legendre[:, :, :coarse]
    coarse_coef = grid_coef[:, ::2]
    band_gauss = lax.dynamic_slice_in_dim(gauss_weights, wave_idx * band_size, band_size)
    local_to = lax.dynamic_slice_in_dim(modes_to, lev_idx * lev_dev, lev_dev, 1)
    local_from = lax.dynamic_slice_in_dim(modes_from, lev_idx * lev_dev, lev_dev, 1)
    mode_decay = lax.dynamic_slice_in_dim(mode_rates, lev_idx * lev_dev, lev_dev)

    def project(partial_sum):
        return mix(modes_to, partial_sum)

    def coarse_start(modes):
        gathered = lax.all_gather(modes, "lev", axis=0, tiled=True)
        levels = (mix(modes_from, gathered) * keep_float).astype(jnp.bfloat16)
        return legendre_inverse(levels, coarse_leg, keep_mask)

    def coarse_grid_step(fourier):
        return grid_step(
            fourier, coarse_table, coarse_coef, band_gauss, 2.0 * coarse / (longitudes // 2)
        )

    def coarse_finish(returned):
        partial_sum = legendre_forward(returned, coarse_leg, keep_mask)
        return lax.psum_scatter(
            project(partial_sum).astype(jnp.bfloat16), "lev", scatter_dimension=0, tiled=True
        ).astype(jnp.float32)

    def coarse_eval(modes):
        fourier = lax.all_to_all(
            coarse_start(modes), "wave", split_axis=5, concat_axis=3, tiled=True
        )
        returned = lax.all_to_all(
            coarse_grid_step(fourier), "wave", split_axis=3, concat_axis=5, tiled=True
        )
        return coarse_finish(returned)

    restricted = fine_state[..., :coarse] * keep_float
    fine_spec = lax.all_gather(fine_state.astype(jnp.bfloat16), "lev", axis=0, tiled=True)
    fine_fourier = legendre_inverse(fine_spec, legendre, member_mask)
    fine_fourier = lax.all_to_all(fine_fourier, "wave", split_axis=5, concat_axis=3, tiled=True)
    fine_back = lax.all_to_all(
        grid_step(fine_fourier, fine_table, grid_coef, band_gauss, 2.0 * fine_width / longitudes),
        "wave",
        split_axis=3,
        concat_axis=5,
        tiled=True,
    )
    fine_tend = lax.psum_scatter(
        legendre_forward(fine_back, legendre, member_mask).astype(jnp.bfloat16),
        "lev",
        scatter_dimension=0,
        tiled=True,
    ).astype(jnp.float32)
    restricted_tend = fine_tend[..., :coarse] * keep_float
    stacked = jnp.concatenate([restricted, restricted_tend], 1)
    both_modes = lax.psum_scatter(
        mix(local_to, stacked).astype(jnp.bfloat16), "lev", scatter_dimension=0, tiled=True
    ).astype(jnp.float32)
    nodes = fine_state.shape[1]
    old_state = both_modes[:, :nodes]
    old_tend = both_modes[:, nodes:]
    old_coarse = coarse_eval(old_state[:, 1:2])
    stiffness = (
        mode_decay[:, None, None, None]
        * (degree * (degree + 1.0) / (coarse * (coarse + 1.0)))[None, None]
    )
    source = old_tend - stiffness[:, None] * old_state
    integral_mid = (
        quad_weights[0][0] * source[:, 0]
        + quad_weights[0][1] * source[:, 1]
        + quad_weights[0][2] * source[:, 2]
    )
    integral_end = (
        quad_weights[1][0] * source[:, 0]
        + quad_weights[1][1] * source[:, 1]
        + quad_weights[1][2] * source[:, 2]
    )
    divisor = 1.0 + STEP_HALF * stiffness
    next_mid = (old_state[:, 0] + STEP_HALF * stiffness * old_state[:, 1] + integral_mid) / divisor
    coarse_fresh = coarse_eval(next_mid[:, None])
    next_end = (
        next_mid
        + STEP_HALF * (coarse_fresh[:, 0] - old_coarse[:, 0])
        + STEP_HALF * stiffness * old_state[:, 2]
        + integral_end
    ) / divisor
    change = jnp.stack([next_mid - old_state[:, 1], next_end - old_state[:, 2]], 1)
    lifted = lax.psum_scatter(
        mix(local_from, change).astype(jnp.bfloat16), "lev", scatter_dimension=0, tiled=True
    ).astype(jnp.float32)
    corrected = fine_state[:, 1:] + jnp.pad(
        lifted, ((0, 0), (0, 0), (0, 0), (0, 0), (0, fine_width + 1 - coarse))
    )
    return (corrected, fine_tend)


LANES = 128
SUBLANES = 8
REPLICATED_BYTES = 16 * 2**20
VMEM_BYTES = 56 * 10**6


def round_up(value, unit):
    return -(-value // unit) * unit


def interpolation(points, targets, degree):
    offset = (
        2.0 * np.pi * (np.arange(targets)[:, None] / targets - np.arange(points)[None, :] / points)
    )
    order = np.arange(1, degree + 1)
    return (1.0 + 2.0 * np.cos(offset[:, :, None] * order).sum(-1)) / points


def wave_rows(waves, points, amplitude):
    turns = np.arange(waves)[:, None] * np.arange(points)[None, :] % points
    angles = turns * (2.0 * np.pi / points)
    return np.concatenate([np.cos(angles), -np.sin(angles)]) * amplitude


def matmul(a, b):
    return jnp.dot(a, b, preferred_element_type=jnp.float32)


def matmul_nt(a, b):
    return lax.dot_general(a, b, (((1,), (1,)), ((), ())), preferred_element_type=jnp.float32)


def matmul_exact(a, b):
    return jnp.dot(a, b, preferred_element_type=jnp.float32, precision=lax.Precision.HIGHEST)


def high_low(values):
    high = values.astype(jnp.bfloat16)
    return high, (values - high.astype(jnp.float32)).astype(jnp.bfloat16)


def matmul_split(left, right):
    high, low = high_low(right)
    return matmul(left, jnp.concatenate([high, low, high], 0))


class Sizes:
    def __init__(self, fine_state, legendre):
        self.n_wave, self.n_lev = lax.axis_size("wave"), lax.axis_size("lev")
        self.lev_dev, self.nodes, _, self.slots, self.fine_rows = fine_state.shape
        self.lats = legendre.shape[1]
        self.n_pair = self.n_lev // 2
        self.fine_width = self.fine_rows - 1
        self.coarse = self.fine_width // 2
        self.levels = self.n_lev * self.lev_dev
        self.dev_rows = self.lev_dev * self.nodes * 2
        self.rows = self.levels * self.nodes * 2
        self.per_node = self.levels * 2
        self.head = self.slots * self.coarse
        self.rest = self.fine_rows - self.coarse
        self.used = self.slots * self.fine_rows
        self.state_rows = round_up(self.dev_rows, SUBLANES)
        self.groups = (self.lats + self.state_rows) // SUBLANES
        self.unit = LANES // self.groups
        self.block_rows = self.lats + SUBLANES + self.state_rows
        self.chips = self.n_wave * self.n_pair
        self.fine_columns = self.n_wave * self.slots * 2
        self.coarse_columns = self.n_wave * self.slots
        self.points = round_up(4 * (self.fine_width - 1) + 1, 32)
        self.coarse_points = round_up(4 * (self.coarse - 1) + 1, 32)


def parts(z):
    narrow = dict(
        wave=(z.points, 2 * z.fine_columns),
        quad=(z.levels * 2 * z.fine_columns, z.points),
        coarse_wave=(z.coarse_points, 2 * z.coarse_columns),
        coarse_quad=(z.levels * 2 * z.coarse_columns, z.coarse_points),
        mix_to=(z.rows, 3 * z.rows),
        mix_from=(z.per_node, 3 * z.per_node),
        mix_back=(z.per_node, 3 * z.per_node),
        lift=(z.lev_dev * (z.nodes - 1) * 2, 3 * (z.nodes - 1) * z.per_node),
    )
    full = dict(
        member=(z.fine_columns, 2 * LANES),
        slot=(z.coarse_columns, LANES),
        keep=(z.n_wave, LANES),
        stiff=(z.n_wave * z.per_node, LANES),
    )

    def placed(shapes, unit):
        out, at = {}, 0
        for name, (count, columns) in shapes.items():
            out[name] = (at, count, columns)
            at += round_up(count, unit)
        return out, (at, max(columns for _, columns in shapes.values()))

    return placed(narrow, 2 * SUBLANES), placed(full, SUBLANES)


class Table:
    def __init__(self, ref, place):
        self.ref, (self.at, self.count, self.columns) = ref, place

    def get(self, begin=0, count=None):
        begin = self.at + begin
        return self.ref[begin : begin + (count or self.count), : self.columns]

    def put(self, values, begin=0):
        begin = self.at + begin
        self.ref[begin : begin + values.shape[0], : self.columns] = values


def named(z, narrow_ref, full_ref):
    (narrow, _), (full, _) = parts(z)
    tables = {name: Table(narrow_ref, place) for name, place in narrow.items()}
    return tables | {name: Table(full_ref, place) for name, place in full.items()}


def copies_in(sources, targets, sems):
    copies = [
        pltpu.make_async_copy(source, target, sems.at[i])
        for i, (source, target) in enumerate(zip(sources, targets))
    ]
    for copy in copies:
        copy.start()
    return copies


def pack_kernel(z, state_hbm, leg_hbm, gauss_hbm, out_ref, state_ref, leg_ref, gauss_ref, sems, rows_s):
    bf, f32 = jnp.bfloat16, jnp.float32
    copies = copies_in((state_hbm, leg_hbm, gauss_hbm), (state_ref, leg_ref, gauss_ref), sems)
    for copy in copies:
        copy.wait()
    row = lax.broadcasted_iota(jnp.int32, (z.fine_rows, LANES), 0)
    lane = lax.broadcasted_iota(jnp.int32, (z.fine_rows, LANES), 1)
    for a in range(z.lev_dev):
        for b in range(z.nodes):
            n = (a * z.nodes + b) * 2
            for s in range(z.slots):
                rows_s[s, n : n + 2, :] = state_ref[a, b, s]
    if z.state_rows > z.dev_rows:
        for s in range(z.slots):
            rows_s[s, z.dev_rows :, :] = jnp.zeros((z.state_rows - z.dev_rows, z.fine_rows), f32)
    table = jnp.zeros((z.lats, LANES), f32)
    state = jnp.zeros((z.state_rows, LANES), f32)
    extra = jnp.zeros((SUBLANES, LANES), f32)
    for s in range(z.slots):
        target = jnp.where(row < z.coarse, s * z.coarse + row, z.head + s * z.rest + row - z.coarse)
        leg = leg_ref[s].astype(f32)
        spec = rows_s[s]
        place = (target == lane).astype(bf)
        table = table + matmul(leg.astype(bf), place)
        state = state + matmul(spec.astype(bf), place)
        if z.head + (s + 1) * z.rest > LANES:
            for q in range(z.groups):
                at = q * SUBLANES
                part = leg[at : at + SUBLANES] if at < z.lats else spec[at - z.lats : at - z.lats + SUBLANES]
                place = ((target >= LANES) & (target - LANES + q * z.unit == lane)).astype(bf)
                extra = extra + matmul(part.astype(bf), place)
    wide_row = lax.broadcasted_iota(jnp.int32, (SUBLANES, z.lats), 0)
    wide_lane = lax.broadcasted_iota(jnp.int32, (SUBLANES, z.lats), 1)
    out_lane = lax.broadcasted_iota(jnp.int32, (SUBLANES, LANES), 1)
    for q in range(z.lats // SUBLANES):
        chosen = jnp.where(wide_lane == wide_row + q * SUBLANES, gauss_ref[...], 0.0)
        column = jnp.sum(chosen, axis=1, keepdims=True)
        high = column.astype(bf).astype(f32)
        at = q * z.unit + z.used - LANES
        extra = extra + jnp.where(out_lane == at, high, 0.0)
        extra = extra + jnp.where(out_lane == at + 1, column - high, 0.0)
    block = jnp.concatenate([table, extra, state], 0).astype(bf)
    for i in range(z.chips):
        out_ref[i] = block


def mix_matrix(pick_left, matrix, pick_right, mask, cut):
    values = matmul_exact(matmul_exact(pick_left, matrix), pick_right) * mask
    high, low = high_low(values)
    lane = lax.broadcasted_iota(jnp.int32, values.shape, 1)
    return jnp.where(lane < cut, high.astype(jnp.float32), low.astype(jnp.float32)).astype(jnp.bfloat16)


def tables_kernel(z, layout, rate_ref, fold_smem, *refs):
    inputs, outputs, scratch = refs[:9], refs[9:11], refs[11:]
    (scaled_s, low_s, sems), staged = scratch[:3], scratch[3:]
    copies = copies_in(inputs, staged, sems)
    fold_ref, coef_ref, basis_ref, spread_ref, coarse_spread_ref = staged[:5]
    sampled_ref, coarse_sampled_ref, matrices_ref, picks_ref = staged[5:]
    out = named(z, *outputs)
    bf, f32 = jnp.bfloat16, jnp.float32
    lev = lax.axis_index("lev")
    core = lax.rem(lev, 2)
    waves, coarse = z.fine_width, z.coarse
    half = z.fine_columns

    for copy in copies[:3]:
        copy.wait()

    def wave_column(count, per_slot):
        row = lax.broadcasted_iota(jnp.int32, (count, z.coarse_columns), 0)
        lane = lax.broadcasted_iota(jnp.int32, (count, z.coarse_columns), 1)
        inside = (row >= lane * per_slot) & (row < (lane + 1) * per_slot)
        small = jnp.sum(jnp.where(inside, fold_ref[...].astype(f32), 0.0), axis=1, keepdims=True)
        if per_slot == 1:
            return small
        first = lax.broadcasted_iota(jnp.int32, (count, 1), 0) & 1
        return jnp.where(first == 0, small, waves - 1 - small)

    def one_hot(count, per_slot, width):
        column = wave_column(count, per_slot)
        lane = lax.broadcasted_iota(jnp.int32, (count, 2 * width), 1).astype(f32)
        top = (lane == column).astype(f32)
        bottom = (lane == column + width).astype(f32)
        return jnp.concatenate([top, bottom], 0).astype(bf)

    hot = one_hot(half, 2, waves)
    coarse_hot = one_hot(z.coarse_columns, 1, coarse)
    tall, short = 2 * waves, 2 * coarse
    table = basis_ref[...].astype(f32)
    for x in range(z.n_pair):
        for o in range(2):
            for al in range(z.lev_dev):
                a = (2 * x + o) * z.lev_dev + al
                level = (2 * x + (core if o == 0 else 1 - core)) * z.lev_dev + al
                scaled = coef_ref[pl.ds(level, 1), :] * table
                scaled_s[a * tall : (a + 1) * tall, :] = scaled.astype(bf)
                low = jnp.concatenate([scaled[:coarse], scaled[waves : waves + coarse]], 0)
                low_s[a * short : (a + 1) * short, :] = low.astype(bf)
    for copy in copies[3:]:
        copy.wait()
    out["wave"].put(matmul_nt(sampled_ref[...], hot).astype(bf))
    out["coarse_wave"].put(matmul_nt(coarse_sampled_ref[...], coarse_hot).astype(bf))
    quad = matmul(scaled_s[...], spread_ref[...]).astype(bf)
    coarse_quad = matmul(low_s[...], coarse_spread_ref[...]).astype(bf)
    for a in range(z.levels):
        values = matmul(hot, quad[a * tall : (a + 1) * tall]).astype(bf)
        out["quad"].put(values, a * values.shape[0])
        values = matmul(coarse_hot, coarse_quad[a * short : (a + 1) * short]).astype(bf)
        out["coarse_quad"].put(values, a * values.shape[0])

    def pick(name, index=0):
        at, rows, columns = layout[name]
        return picks_ref[pl.ds(pl.multiple_of(at + index * rows, SUBLANES), rows), :columns]

    def mix(left, matrix, right, mask):
        return mix_matrix(left, matrices_ref[matrix], right, mask, right.shape[1] // 3 * 2)

    out["mix_to"].put(mix(pick("to_left"), 1, pick("to_right", core), pick("to_mask")))
    out["mix_from"].put(mix(pick("from_left", core), 0, pick("from_right"), pick("from_mask")))
    out["mix_back"].put(mix(pick("back_left"), 1, pick("back_right", core), pick("from_mask")))
    out["lift"].put(mix(pick("lift_left", lev), 0, pick("lift_right"), pick("lift_mask")))

    wide = 2 * LANES
    lane = lax.broadcasted_iota(jnp.int32, (1, wide), 1)
    lane_slot = jnp.full((1, wide), -1, jnp.int32)
    lane_row = jnp.zeros((1, wide), jnp.int32)
    for s in range(z.slots):
        for begin, width, first in ((s * coarse, coarse, 0), (z.head + s * z.rest, z.rest, coarse)):
            inside = (lane >= begin) & (lane < begin + width)
            lane_slot = jnp.where(inside, s, lane_slot)
            lane_row = jnp.where(inside, lane - begin + first, lane_row)
    rate_row = lax.broadcasted_iota(jnp.int32, (z.per_node, LANES), 0)
    rates = jnp.zeros((z.per_node, LANES), f32)
    for q in range(z.levels):
        rates = jnp.where((rate_row >= 2 * q) & (rate_row < 2 * q + 2), rate_ref[q], rates)
    for w in range(z.n_wave):
        small = jnp.zeros((1, wide), jnp.int32)
        for s in range(z.slots):
            small = jnp.where(lane_slot == s, fold_smem[w * z.slots + s], small)
        first = lane_row < waves - small
        keep = (lane < z.head) & (lane_row < coarse - small)
        out["keep"].put(keep[:, :LANES].astype(f32), w)
        for s in range(z.slots):
            own = lane_slot == s
            at = (w * z.slots + s) * 2
            out["member"].put((own & first).astype(f32), at)
            out["member"].put((own & jnp.logical_not(first)).astype(f32), at + 1)
            out["slot"].put((own & keep)[:, :LANES].astype(f32), w * z.slots + s)
        degree = (small + lane_row)[:, :LANES].astype(f32)
        stiff = rates * (degree * (degree + 1.0) / (coarse * (coarse + 1.0)))
        out["stiff"].put(stiff, w * z.per_node)


def sweep_kernel(
    z,
    own_ref,
    other_ref,
    state_ref,
    narrow_hbm,
    full_hbm,
    corrected_ref,
    tend_ref,
    leg_s,
    state_s,
    fourier_s,
    back_s,
    tend_s,
    coarse_s,
    coarse_back_s,
    change_s,
    narrow_ref,
    full_ref,
    sems,
):
    bf, f32 = jnp.bfloat16, jnp.float32
    slots, rows, lats, per_node = z.slots, z.rows, z.lats, z.per_node
    table = named(z, narrow_ref, full_ref)
    copies = copies_in((full_hbm, narrow_hbm), (full_ref, narrow_ref), sems)
    wide = 2 * LANES
    all_lats = z.n_lev * lats

    def member(w, j):
        return table["member"].get(w * slots * 2 + j, 1)

    def slot(w, s):
        return table["slot"].get(w * slots + s, 1)

    def keep(w):
        return table["keep"].get(w, 1)

    for w in range(z.n_wave):
        for x in range(z.n_pair):
            for o, ref in enumerate((own_ref, other_ref)):
                d = 2 * x + o
                block = ref[w * z.n_pair + x].astype(f32)
                extra = block[lats : lats + SUBLANES]
                leg_s[w, d * lats : (d + 1) * lats, :LANES] = block[:lats]
                state_at = d * z.dev_rows
                begin = lats + SUBLANES
                state_s[w, state_at : state_at + z.dev_rows, :LANES] = block[begin : begin + z.dev_rows]
                for q in range(z.groups):
                    moved = extra if q == 0 else pltpu.roll(extra, LANES - q * z.unit, 1)
                    at = q * SUBLANES
                    if at < lats:
                        leg_s[w, d * lats + at : d * lats + at + SUBLANES, LANES:] = moved
                    else:
                        at = at - lats
                        count = min(SUBLANES, z.dev_rows - at)
                        state_s[w, state_at + at : state_at + at + count, LANES:] = moved[:count]
        if all_lats < leg_s.shape[1]:
            leg_s[w, all_lats:, :] = jnp.zeros((leg_s.shape[1] - all_lats, wide), f32)

    def legendre(w):
        return leg_s[w].astype(bf)

    def weighted(w):
        values = leg_s[w]
        column = values[:, z.used : z.used + 1] + values[:, z.used + 1 : z.used + 2]
        return (values * column).astype(bf)

    copies[0].wait()
    for w in range(z.n_wave):
        state = state_s[w]
        left = jnp.concatenate([state * member(w, j) for j in range(2 * slots)], 0).astype(bf)
        out = matmul_nt(left, legendre(w))
        for j in range(2 * slots):
            fourier_s[pl.ds(w * 2 * slots + j, rows, stride=z.fine_columns), :] = out[j * rows : (j + 1) * rows]

    copies[1].wait()
    both = 2 * z.fine_columns
    for a in range(z.levels):
        pieces = [
            fourier_s[(a * z.nodes + b) * both : (a * z.nodes + b + 1) * both, :].astype(bf)
            for b in range(z.nodes)
        ]
        grid = matmul(table["wave"].get(), jnp.concatenate(pieces, 1))
        product = (grid * grid).astype(bf)
        back = matmul(table["quad"].get(a * both, both), product)
        for b in range(z.nodes):
            back_s[(a * z.nodes + b) * both : (a * z.nodes + b + 1) * both, :] = back[:, b * LANES : (b + 1) * LANES]

    stacked = []
    for w in range(z.n_wave):
        left = jnp.concatenate(
            [
                back_s[pl.ds(w * 2 * slots + j, rows, stride=z.fine_columns), :].astype(bf)
                for j in range(2 * slots)
            ],
            0,
        )
        out = matmul(left, weighted(w))
        total = member(w, 0) * out[:rows]
        for j in range(1, 2 * slots):
            total = total + member(w, j) * out[j * rows : (j + 1) * rows]
        tend_s[w, :rows, :] = total
        stacked.append(state_s[w][:, :LANES] * keep(w))
        stacked.append(total[:, :LANES] * keep(w))

    modes = matmul_split(table["mix_to"].get(), jnp.concatenate(stacked, 1))
    evals, later, old_of, mid_of = [], [], [], []
    for w in range(z.n_wave):
        old, source = [], []
        stiff = table["stiff"].get(w * per_node, per_node)
        for b in range(z.nodes):
            part = modes[b * per_node : (b + 1) * per_node]
            old.append(part[:, 2 * w * LANES : (2 * w + 1) * LANES])
            source.append(part[:, (2 * w + 1) * LANES : (2 * w + 2) * LANES] - stiff * old[-1])
        divisor = 1.0 + STEP_HALF * stiff
        mid = sum(quad_weights[0][b] * source[b] for b in range(z.nodes))
        mid = (mid + old[0] + STEP_HALF * stiff * old[1]) / divisor
        end = sum(quad_weights[1][b] * source[b] for b in range(z.nodes))
        end = end + mid + STEP_HALF * stiff * old[2]
        evals.append(old[1])
        evals.append(mid)
        later.append((end, divisor))
        old_of.append(old)
        mid_of.append(mid)

    level_values = matmul_split(table["mix_from"].get(), jnp.concatenate(evals, 1))
    for w in range(z.n_wave):
        left = jnp.concatenate(
            [
                level_values[:, (2 * w + e) * LANES : (2 * w + e + 1) * LANES] * slot(w, s)
                for s in range(slots)
                for e in range(2)
            ],
            0,
        ).astype(bf)
        out = matmul_nt(left, legendre(w)[:, :LANES])
        for s in range(slots):
            for e in range(2):
                at = (s * 2 + e) * per_node
                coarse_s[e, pl.ds(w * slots + s, per_node, stride=z.coarse_columns), :] = out[at : at + per_node]

    both_c = 2 * z.coarse_columns
    for a in range(z.levels):
        pieces = [coarse_s[e, a * both_c : (a + 1) * both_c, :].astype(bf) for e in range(2)]
        grid = matmul(table["coarse_wave"].get(), jnp.concatenate(pieces, 1))
        product = (grid * grid).astype(bf)
        back = matmul(table["coarse_quad"].get(a * both_c, both_c), product)
        for e in range(2):
            coarse_back_s[e, a * both_c : (a + 1) * both_c, :] = back[:, e * LANES : (e + 1) * LANES]

    tends = []
    for w in range(z.n_wave):
        left = jnp.concatenate(
            [
                coarse_back_s[e, pl.ds(w * slots + s, per_node, stride=z.coarse_columns), :].astype(bf)
                for s in range(slots)
                for e in range(2)
            ],
            0,
        )
        out = matmul(left, weighted(w)[:, :LANES])
        for e in range(2):
            total = None
            for s in range(slots):
                at = (s * 2 + e) * per_node
                term = slot(w, s) * out[at : at + per_node]
                total = term if total is None else total + term
            tends.append(total)
    coarse_modes = matmul_split(table["mix_back"].get(), jnp.concatenate(tends, 1))
    for w in range(z.n_wave):
        before = coarse_modes[:, 2 * w * LANES : (2 * w + 1) * LANES]
        fresh = coarse_modes[:, (2 * w + 1) * LANES : (2 * w + 2) * LANES]
        end, divisor = later[w]
        end = (end + STEP_HALF * (fresh - before)) / divisor
        change_s[w, :per_node, :] = mid_of[w] - old_of[w][1]
        change_s[w, per_node:, :] = end - old_of[w][2]

    place = lax.axis_index("wave")
    begin = pl.multiple_of(lax.div(lax.axis_index("lev"), 2) * (2 * z.dev_rows), SUBLANES)
    mine = tend_s[place, pl.ds(begin, z.state_rows), :]
    raised = matmul_split(table["lift"].get(), change_s[place])
    lane = lax.broadcasted_iota(jnp.int32, (z.state_rows, wide), 1)
    for s in range(slots):
        low = mine if s == 0 else pltpu.roll(mine, wide - s * z.coarse, 1)
        high = pltpu.roll(mine, wide - (z.head + s * z.rest - z.coarse), 1)
        values = jnp.where(lane < z.coarse, low, high)
        for n in range(0, z.dev_rows, 2):
            tend_ref[n // (z.nodes * 2), n // 2 % z.nodes, s] = values[n : n + 2, : z.fine_rows]
        low = raised if s == 0 else pltpu.roll(raised, LANES - s * z.coarse, 1)
        low = jnp.where(lane[: low.shape[0], :LANES] < z.coarse, low, 0.0)
        for n in range(0, low.shape[0], 2):
            a, b = n // (2 * (z.nodes - 1)), n // 2 % (z.nodes - 1)
            corrected_ref[a, b, s] = state_ref[a, b + 1, s] + low[n : n + 2, : z.fine_rows]


def mix_constants(z):
    level, node, part = np.arange(z.levels), np.arange(z.nodes), np.arange(2)

    def pick(index):
        return (np.asarray(index)[:, None] == level[None, :]).astype(np.float32)

    def grid(*axes):
        return [m.reshape(-1) for m in np.meshgrid(*axes, indexing="ij")]

    def ordered(index, core):
        lev, inner = index // z.lev_dev, index % z.lev_dev
        return (lev ^ core) * z.lev_dev + inner

    def thrice(matrix):
        return np.concatenate([matrix] * 3, -1)

    rb, rq, rc = grid(node, level, part)
    ca, cb, cc = grid(level, node, part)
    sa, sc = grid(level, part)
    to_mask = (rb[:, None] == cb[None]) & (rc[:, None] == cc[None])
    same_part = sc[:, None] == sc[None]
    la, lb, lc = grid(np.arange(z.lev_dev), np.arange(z.nodes - 1), part)
    kb, kq, kc = grid(np.arange(z.nodes - 1), level, part)
    lift_mask = (lb[:, None] == kb[None]) & (lc[:, None] == kc[None])
    by_core = range(2)
    constants = dict(
        to_left=[pick(rq)],
        to_right=[thrice(pick(ordered(ca, k)).T) for k in by_core],
        to_mask=[thrice(to_mask)],
        from_left=[pick(ordered(sa, k)) for k in by_core],
        from_right=[thrice(pick(sa).T)],
        from_mask=[thrice(same_part)],
        back_left=[pick(sa)],
        back_right=[thrice(pick(ordered(sa, k)).T) for k in by_core],
        lift_left=[pick(k * z.lev_dev + la) for k in range(z.n_lev)],
        lift_right=[thrice(pick(kq).T)],
        lift_mask=[thrice(lift_mask)],
    )
    wide = max(m[0].shape[1] for m in constants.values())
    layout, rows, at = {}, [], 0
    for name, members in constants.items():
        count, columns = members[0].shape
        height = round_up(count, SUBLANES)
        layout[name] = (at, height, columns)
        at += height * len(members)
        rows += [np.pad(m, ((0, height - count), (0, wide - columns))) for m in members]
    return layout, jnp.asarray(np.concatenate(rows), jnp.float32)


def replicated_plan(
    fine_state, fold_pairs, legendre, gauss_weights, grid_coef, modes_from, modes_to, mode_rates
):
    z = Sizes(fine_state, legendre)
    bf, f32 = jnp.bfloat16, jnp.float32
    longitudes = grid_coef.shape[1]
    vmem = pl.BlockSpec(memory_space=pltpu.VMEM)
    smem = pl.BlockSpec(memory_space=pltpu.SMEM)
    hbm = pl.BlockSpec(memory_space=pltpu.HBM)
    shape = jax.ShapeDtypeStruct
    stored = jnp.swapaxes(fine_state, 2, 3)
    block = pl.pallas_call(
        functools.partial(pack_kernel, z),
        out_shape=shape((z.chips, z.block_rows, LANES), bf),
        in_specs=[hbm] * 3,
        out_specs=vmem,
        scratch_shapes=[
            pltpu.VMEM(stored.shape, f32),
            pltpu.VMEM(legendre.shape, bf),
            pltpu.VMEM((1, z.lats), f32),
            pltpu.SemaphoreType.DMA((3,)),
            pltpu.VMEM((z.slots, z.state_rows, z.fine_rows), f32),
        ],
        name="pack",
    )(stored, legendre, gauss_weights[None])
    groups = [[2 * i + c for i in range(z.chips)] for c in range(2)]
    own = lax.all_to_all(
        block, ("wave", "lev"), 0, 0, tiled=True, axis_index_groups=groups
    )
    fine_amp, coarse_amp = z.fine_width**-0.5, z.coarse**-0.5
    basis = wave_rows(z.fine_width, longitudes, fine_amp)
    spread = interpolation(z.points, longitudes, 2 * (z.fine_width - 1))
    spread *= 2.0 * z.fine_width / longitudes
    coarse_spread = interpolation(z.coarse_points, longitudes, 2 * (z.coarse - 1))
    coarse_spread *= 2.0 * z.coarse / (longitudes // 2) * (coarse_amp / fine_amp)
    coarse_spread[1::2] = 0.0
    sampled = wave_rows(z.fine_width, z.points, fine_amp).T
    coarse_sampled = wave_rows(z.coarse, z.coarse_points, coarse_amp).T
    constants = [jnp.asarray(c, bf) for c in (basis, spread, coarse_spread, sampled, coarse_sampled)]
    layout, picks = mix_constants(z)
    staged = [fold_pairs[None], grid_coef, *constants, jnp.stack([modes_from, modes_to]), picks]
    wide = 2 * LANES
    (_, narrow_shape), (_, full_shape) = parts(z)
    tables = pl.pallas_call(
        functools.partial(tables_kernel, z, layout),
        out_shape=(shape(narrow_shape, bf), shape(full_shape, f32)),
        in_specs=[smem, smem] + [hbm] * len(staged),
        out_specs=(vmem,) * 2,
        scratch_shapes=[
            pltpu.VMEM((z.levels * 2 * z.fine_width, longitudes), bf),
            pltpu.VMEM((z.levels * 2 * z.coarse, longitudes), bf),
            pltpu.SemaphoreType.DMA((len(staged),)),
        ]
        + [pltpu.VMEM(array.shape, array.dtype) for array in staged],
        cost_estimate=pl.CostEstimate(flops=10**9, bytes_accessed=4 * 10**6, transcendentals=0),
        name="tables",
    )(mode_rates, fold_pairs, *staged)

    own, *tables = lax.optimization_barrier((own, *tables))
    other = lax.ppermute(own, ("wave", "lev"), [(i, i ^ 1) for i in range(2 * z.chips)])

    lat_rows = round_up(z.n_lev * z.lats, LANES)
    corrected, fine_tend = pl.pallas_call(
        functools.partial(sweep_kernel, z),
        out_shape=(
            shape((z.lev_dev, z.nodes - 1, z.slots, 2, z.fine_rows), f32),
            shape(stored.shape, f32),
        ),
        in_specs=[vmem] * 3 + [hbm] * 2,
        out_specs=(vmem, vmem),
        scratch_shapes=[
            pltpu.VMEM((z.n_wave, lat_rows, wide), f32),
            pltpu.VMEM((z.n_wave, z.rows, wide), f32),
            pltpu.VMEM((z.rows * z.fine_columns, lat_rows), f32),
            pltpu.VMEM((z.rows * z.fine_columns, lat_rows), f32),
            pltpu.VMEM((z.n_wave, z.rows + SUBLANES, wide), f32),
            pltpu.VMEM((2, z.per_node * z.coarse_columns, lat_rows), f32),
            pltpu.VMEM((2, z.per_node * z.coarse_columns, lat_rows), f32),
            pltpu.VMEM((z.n_wave, (z.nodes - 1) * z.per_node, LANES), f32),
            pltpu.VMEM(narrow_shape, bf),
            pltpu.VMEM(full_shape, f32),
            pltpu.SemaphoreType.DMA((2,)),
        ],
        compiler_params=pltpu.CompilerParams(vmem_limit_bytes=VMEM_BYTES),
        name="sweep",
    )(own, other, stored, *tables)
    return (jnp.swapaxes(corrected, 2, 3), jnp.swapaxes(fine_tend, 2, 3))


def fits_replicated(fine_state, legendre):
    n_wave, n_lev = lax.axis_size("wave"), lax.axis_size("lev")
    if n_lev % 2 or fine_state.shape[1] != len(quad_weights[0]):
        return False
    z = Sizes(fine_state, legendre)
    gathered = 32 * n_wave * n_lev * (legendre.size + fine_state.size)
    return (
        z.head <= LANES
        and z.used > LANES
        and z.used + 2 - LANES <= z.unit
        and z.lats % SUBLANES == 0
        and n_lev * z.lats <= LANES
        and gathered <= REPLICATED_BYTES
    )


def per_device(fine_state, fold_pairs, legendre, *rest):
    plan = replicated_plan if fits_replicated(fine_state, legendre) else split_plan
    return plan(fine_state, fold_pairs, legendre, *rest)


def solution(mesh):
    placed = (
        P("lev", None, None, "wave", None),
        P(),
        P("wave", "lev", None),
        P("lev"),
        P(),
        P(),
        P(),
        P(),
    )
    return jax.shard_map(
        per_device,
        mesh=mesh,
        in_specs=placed,
        out_specs=(P("lev", None, None, "wave", None), P("lev", None, None, "wave", None)),
        check_vma=False,
    )
```

profile of v0, /device:TPU:0, one launch (start us, length us, event | category | flops | bytes accessed | tf_op | source)
XLA Modules:
  0.0 27.5 jit_solution(1245872430474726019)
XLA Ops:
  0.6 1.6 %pack.1 = bf16[16,48,128]{2,1,0:T(8,128)(2,1)} custom-call(f32[2,3,3,2,49]{4,3,2,1,0:T(2,128)} %bitcast.7, bf16[3,24,49]{2,1,0:T(8,128)(2,1)} %leg_hbm.1, f32[1,24]{1,0:T(1,128)} %bitcast.11), custom_call_target="tpu_custom_call" | custom-call | tf_op jit(solution)/shard_map/pack/pallas_call | solution.py:722
  2.3 8.4 %all-to-all-start = ((bf16[16,48,128]{2,1,0:T(8,128)(2,1)}), bf16[16,48,128]{2,1,0:T(8,128)(2,1)S(1)}, u32[]{:S(2)}, u32[]{:S(2)}) async-start(bf16[16,48,128]{2,1,0:T(8,128)(2,1)} %pack.1), calls=%async_computation | async-start | bytes 393216 | tf_op jit(solution)/shard_map/all_to_all | solution.py:737
  10.6 1.3 %pad_maximum_fusion.refs_7_ = f32[2,8,8]{2,1,0:T(8,128)} fusion(f32[1,8,8]{2,1,0:T(8,128)} %bitcast.9, f32[1,8,8]{2,1,0:T(8,128)} %bitcast.10), kind=kLoop, calls=%fused_computation | loop fusion | flops 128 | bytes 1024 | tf_op jit(solution)/shard_map/stack | solution.py:751
  11.9 0.0 copy-start
  11.9 6.5 %tables.1 = (bf16[1536,192]{1,0:T(8,128)(2,1)}, f32[208,256]{1,0:T(8,128)}) custom-call(f32[8]{0:T(128)} %rate_ref.1, s32[24]{0:T(128)} %fold_smem.1, s32[1,24]{1,0:T(1,128)} %bitcast.14, f32[8,2560]{1,0:T(8,128)} %refs_1_.1, bf16[96,2560]{1,0:T(8,128)(2,1)} %constant.12.clone.refs_2_, bf16[2560,192]{1,0:T(8,128)(2,1)} %constant.13.clone.refs_3_, ...), custom_call_target="tpu_custom_call" | custom-call | flops 1000000000 | bytes 4000000 | tf_op jit(solution)/shard_map/tables/pallas_call | solution.py:754
  18.5 0.8 %all-to-all-done.own_ref = bf16[16,48,128]{2,1,0:T(8,128)(2,1)S(1)} async-done(((bf16[16,48,128]{2,1,0:T(8,128)(2,1)}), bf16[16,48,128]{2,1,0:T(8,128)(2,1)S(1)}, u32[]{:S(2)}, u32[]{:S(2)}) %all-to-all-start) | async-done | bytes 196640 | tf_op jit(solution)/shard_map/all_to_all | solution.py:737
  19.3 0.0 collective-permute-start
  19.3 1.4 %collective-permute-done.other_ref = bf16[16,48,128]{2,1,0:T(8,128)(2,1)S(1)} collective-permute-done((bf16[16,48,128]{2,1,0:T(8,128)(2,1)S(1)}, bf16[16,48,128]{2,1,0:T(8,128)(2,1)S(1)}, u32[]{:S(2)}, u32[]{:S(2)}) %collective-permute-start) | collective-permute-done | bytes 196640 | tf_op jit(solution)/shard_map/ppermute | solution.py:770
  20.7 0.0 copy-done
  20.7 6.8 %sweep.1 = (f32[2,2,3,2,49]{4,3,2,1,0:T(2,128)}, f32[2,3,3,2,49]{4,3,2,1,0:T(2,128)}) custom-call(bf16[16,48,128]{2,1,0:T(8,128)(2,1)S(1)} %all-to-all-done.own_ref, bf16[16,48,128]{2,1,0:T(8,128)(2,1)S(1)} %collective-permute-done.other_ref, f32[2,3,3,2,49]{4,3,2,1,0:T(2,128)S(1)} %bitcast.8, bf16[1536,192]{1,0:T(8,128)(2,1)} %get-tuple-element.12.narrow_hbm, ...), custom_call_target="tpu_custom_call" | custom-call | tf_op jit(solution)/shard_map/sweep/pallas_call | solution.py:773
Async XLA Ops:
  2.3 17.0 %all-to-all-start = ((bf16[16,48,128]{2,1,0:T(8,128)(2,1)}), bf16[16,48,128]{2,1,0:T(8,128)(2,1)S(1)}, u32[]{:S(2)}, u32[]{:S(2)}) async-start(bf16[16,48,128]{2,1,0:T(8,128)(2,1)} %pack.1), calls=%async_computation | async-start | bytes 393216 | tf_op jit(solution)/shard_map/all_to_all | solution.py:737
  11.9 8.8 %copy-start = (f32[2,3,2,3,49]{4,2,3,1,0:T(2,128)S(1)}, f32[2,3,2,3,49]{4,2,3,1,0:T(2,128)}, u32[]{:S(2)}) copy-start(f32[2,3,2,3,49]{4,2,3,1,0:T(2,128)} %param.14) | copy-start | bytes 21172
  19.3 1.4 %collective-permute-start = (bf16[16,48,128]{2,1,0:T(8,128)(2,1)S(1)}, bf16[16,48,128]{2,1,0:T(8,128)(2,1)S(1)}, u32[]{:S(2)}, u32[]{:S(2)}) collective-permute-start(bf16[16,48,128]{2,1,0:T(8,128)(2,1)S(1)} %all-to-all-done.own_ref), channel_id=1, source_target_pairs={{0,1},{1,0},{2,3},{3,2},{4,5},{5,4},{6,7},{7,6},{8,9},{9,8},{10,11... | collective-permute-start | bytes 589832 | tf_op jit(solution)/shard_map/ppermute | solution.py:770
where the time goes:
time: 27.9 us; the launch traced here: 27.5 us
  Pallas kernels  14.9 us (53%)
  starting transfers between devices  8.36 us (30%)
  waiting for transfers between devices  2.26 us (8%)
  other arithmetic  1.31 us (5%)
  between operations  0.66 us (2%)
    all_to_all x1, starting transfers between devices, replicated_plan(): lax.all_to_all(block, ('wave', 'lev'), 0, 0, tiled=True, axis_index_group...  8.35 us
    pallas_call x1, Pallas kernels, replicated_plan(): pl.pallas_call(functools.partial(sweep_kernel, z), out_shape=(shape((z.le...  6.79 us
    pallas_call x1, Pallas kernels, replicated_plan(): pl.pallas_call(functools.partial(tables_kernel, z, layout), out_shape=(sh...  6.5 us
    pallas_call x1, Pallas kernels, replicated_plan(): pl.pallas_call(functools.partial(pack_kernel, z), out_shape=shape((z.chip...  1.63 us
    ppermute x1, waiting for transfers between devices, replicated_plan(): lax.ppermute(own, ('wave', 'lev'), [(i, i ^ 1) for i in range(2 * z.chips)])  1.44 us
    another operation x1, other arithmetic, replicated_plan(): jnp.stack([modes_from, modes_to])  1.31 us
    all_to_all x1, waiting for transfers between devices, replicated_plan(): lax.all_to_all(block, ('wave', 'lev'), 0, 0, tiled=True, axis_index_group...  0.82 us
  transfers between devices with their start and end apart: 2, of which 2 were waited for; matrix products, arithmetic and copies ran while one was open for 5% of the time, Pallas kernels for 24%

commit v1 on v0

--- a/solution.py
+++ b/solution.py
@@ -269,6 +269,7 @@
         slot=(z.coarse_columns, LANES),
         keep=(z.n_wave, LANES),
         stiff=(z.n_wave * z.per_node, LANES),
+        inverse=(z.n_wave * z.per_node, LANES),
     )
 
     def placed(shapes, unit):
@@ -364,11 +365,11 @@
 
 
 def tables_kernel(z, layout, rate_ref, fold_smem, *refs):
-    inputs, outputs, scratch = refs[:9], refs[9:11], refs[11:]
-    (scaled_s, low_s, sems), staged = scratch[:3], scratch[3:]
+    inputs, outputs, scratch = refs[:10], refs[10:12], refs[12:]
+    (scaled_s, sems), staged = scratch[:2], scratch[2:]
     copies = copies_in(inputs, staged, sems)
     fold_ref, coef_ref, basis_ref, spread_ref, coarse_spread_ref = staged[:5]
-    sampled_ref, coarse_sampled_ref, matrices_ref, picks_ref = staged[5:]
+    sampled_ref, coarse_sampled_ref, from_ref, to_ref, picks_ref = staged[5:]
     out = named(z, *outputs)
     bf, f32 = jnp.bfloat16, jnp.float32
     lev = lax.axis_index("lev")
@@ -392,31 +393,38 @@
     def one_hot(count, per_slot, width):
         column = wave_column(count, per_slot)
         lane = lax.broadcasted_iota(jnp.int32, (count, 2 * width), 1).astype(f32)
-        top = (lane == column).astype(f32)
-        bottom = (lane == column + width).astype(f32)
-        return jnp.concatenate([top, bottom], 0).astype(bf)
+        extra = width - coarse
+        top = lane == jnp.where(column < coarse, column, column + coarse)
+        bottom = lane == jnp.where(column < coarse, column + coarse, column + coarse + extra)
+        return jnp.concatenate([top.astype(f32), bottom.astype(f32)], 0).astype(bf)
 
     hot = one_hot(half, 2, waves)
     coarse_hot = one_hot(z.coarse_columns, 1, coarse)
-    tall, short = 2 * waves, 2 * coarse
-    table = basis_ref[...].astype(f32)
-    for x in range(z.n_pair):
-        for o in range(2):
-            for al in range(z.lev_dev):
-                a = (2 * x + o) * z.lev_dev + al
-                level = (2 * x + (core if o == 0 else 1 - core)) * z.lev_dev + al
-                scaled = coef_ref[pl.ds(level, 1), :] * table
-                scaled_s[a * tall : (a + 1) * tall, :] = scaled.astype(bf)
-                low = jnp.concatenate([scaled[:coarse], scaled[waves : waves + coarse]], 0)
-                low_s[a * short : (a + 1) * short, :] = low.astype(bf)
+    short, long = 2 * coarse, 2 * (waves - coarse)
+    levels = [
+        (2 * x + (core if o == 0 else 1 - core)) * z.lev_dev + al
+        for x in range(z.n_pair)
+        for o in range(2)
+        for al in range(z.lev_dev)
+    ]
+    chunk = 2 * LANES
+    for begin in range(0, basis_ref.shape[1], chunk):
+        values = basis_ref[:, begin : begin + chunk].astype(f32)
+        for a, level in enumerate(levels):
+            scaled = coef_ref[pl.ds(level, 1), begin : begin + chunk] * values
+            scaled_s[a * short : (a + 1) * short, begin : begin + chunk] = scaled[:short].astype(bf)
+            at = z.levels * short + a * long
+            scaled_s[at : at + long, begin : begin + chunk] = scaled[short:].astype(bf)
     for copy in copies[3:]:
         copy.wait()
     out["wave"].put(matmul_nt(sampled_ref[...], hot).astype(bf))
     out["coarse_wave"].put(matmul_nt(coarse_sampled_ref[...], coarse_hot).astype(bf))
+    coarse_quad = matmul(scaled_s[: z.levels * short, :], coarse_spread_ref[...]).astype(bf)
     quad = matmul(scaled_s[...], spread_ref[...]).astype(bf)
-    coarse_quad = matmul(low_s[...], coarse_spread_ref[...]).astype(bf)
     for a in range(z.levels):
-        values = matmul(hot, quad[a * tall : (a + 1) * tall]).astype(bf)
+        at = z.levels * short + a * long
+        pair = jnp.concatenate([quad[a * short : (a + 1) * short], quad[at : at + long]], 0)
+        values = matmul(hot, pair).astype(bf)
         out["quad"].put(values, a * values.shape[0])
         values = matmul(coarse_hot, coarse_quad[a * short : (a + 1) * short]).astype(bf)
         out["coarse_quad"].put(values, a * values.shape[0])
@@ -426,12 +434,12 @@
         return picks_ref[pl.ds(pl.multiple_of(at + index * rows, SUBLANES), rows), :columns]
 
     def mix(left, matrix, right, mask):
-        return mix_matrix(left, matrices_ref[matrix], right, mask, right.shape[1] // 3 * 2)
-
-    out["mix_to"].put(mix(pick("to_left"), 1, pick("to_right", core), pick("to_mask")))
-    out["mix_from"].put(mix(pick("from_left", core), 0, pick("from_right"), pick("from_mask")))
-    out["mix_back"].put(mix(pick("back_left"), 1, pick("back_right", core), pick("from_mask")))
-    out["lift"].put(mix(pick("lift_left", lev), 0, pick("lift_right"), pick("lift_mask")))
+        return mix_matrix(left, matrix[...], right, mask, right.shape[1] // 3 * 2)
+
+    out["mix_to"].put(mix(pick("to_left"), to_ref, pick("to_right", core), pick("to_mask")))
+    out["mix_from"].put(mix(pick("from_left", core), from_ref, pick("from_right"), pick("from_mask")))
+    out["mix_back"].put(mix(pick("back_left"), to_ref, pick("back_right", core), pick("from_mask")))
+    out["lift"].put(mix(pick("lift_left", lev), from_ref, pick("lift_right"), pick("lift_mask")))
 
     wide = 2 * LANES
     lane = lax.broadcasted_iota(jnp.int32, (1, wide), 1)
@@ -462,6 +470,7 @@
         degree = (small + lane_row)[:, :LANES].astype(f32)
         stiff = rates * (degree * (degree + 1.0) / (coarse * (coarse + 1.0)))
         out["stiff"].put(stiff, w * z.per_node)
+        out["inverse"].put(1.0 / (1.0 + STEP_HALF * stiff), w * z.per_node)
 
 
 def sweep_kernel(
@@ -484,6 +493,9 @@
     narrow_ref,
     full_ref,
     sems,
+    legendre_s,
+    product_s,
+    coarse_product_s,
 ):
     bf, f32 = jnp.bfloat16, jnp.float32
     slots, rows, lats, per_node = z.slots, z.rows, z.lats, z.per_node
@@ -522,35 +534,34 @@
                         state_s[w, state_at + at : state_at + at + count, LANES:] = moved[:count]
         if all_lats < leg_s.shape[1]:
             leg_s[w, all_lats:, :] = jnp.zeros((leg_s.shape[1] - all_lats, wide), f32)
-
-    def legendre(w):
-        return leg_s[w].astype(bf)
-
-    def weighted(w):
-        values = leg_s[w]
-        column = values[:, z.used : z.used + 1] + values[:, z.used + 1 : z.used + 2]
-        return (values * column).astype(bf)
+        legendre_s[w] = leg_s[w].astype(bf)
+
+    lane = lax.broadcasted_iota(jnp.int32, (2 * SUBLANES, wide), 1)
+    picked = ((lane == z.used) | (lane == z.used + 1)).astype(bf)
+    gauss = matmul_nt(picked, legendre_s[0])[:1]
 
     copies[0].wait()
     for w in range(z.n_wave):
         state = state_s[w]
         left = jnp.concatenate([state * member(w, j) for j in range(2 * slots)], 0).astype(bf)
-        out = matmul_nt(left, legendre(w))
-        for j in range(2 * slots):
-            fourier_s[pl.ds(w * 2 * slots + j, rows, stride=z.fine_columns), :] = out[j * rows : (j + 1) * rows]
+        fourier_s[w * 2 * slots * rows : (w + 1) * 2 * slots * rows, :] = matmul_nt(left, legendre_s[w])
 
     copies[1].wait()
     both = 2 * z.fine_columns
+    half = z.fine_columns
     for a in range(z.levels):
-        pieces = [
-            fourier_s[(a * z.nodes + b) * both : (a * z.nodes + b + 1) * both, :].astype(bf)
-            for b in range(z.nodes)
-        ]
+        pieces = []
+        for b in range(z.nodes):
+            at = (a * z.nodes + b) * 2
+            piece = [fourier_s[pl.ds(at + c, half, stride=rows), :] for c in range(2)]
+            pieces.append(jnp.concatenate(piece, 0).astype(bf))
         grid = matmul(table["wave"].get(), jnp.concatenate(pieces, 1))
-        product = (grid * grid).astype(bf)
-        back = matmul(table["quad"].get(a * both, both), product)
+        product_s[a] = (grid * grid).astype(bf)
+    for a in range(z.levels):
+        back = matmul(table["quad"].get(a * both, both), product_s[a])
         for b in range(z.nodes):
-            back_s[(a * z.nodes + b) * both : (a * z.nodes + b + 1) * both, :] = back[:, b * LANES : (b + 1) * LANES]
+            values = back[:, b * LANES : (b + 1) * LANES] * gauss
+            back_s[(a * z.nodes + b) * both : (a * z.nodes + b + 1) * both, :] = values
 
     stacked = []
     for w in range(z.n_wave):
@@ -561,10 +572,10 @@
             ],
             0,
         )
-        out = matmul(left, weighted(w))
-        total = member(w, 0) * out[:rows]
+        out = matmul(left, legendre_s[w])
+        total = out[:rows]
         for j in range(1, 2 * slots):
-            total = total + member(w, j) * out[j * rows : (j + 1) * rows]
+            total = jnp.where(member(w, j) > 0.5, out[j * rows : (j + 1) * rows], total)
         tend_s[w, :rows, :] = total
         stacked.append(state_s[w][:, :LANES] * keep(w))
         stacked.append(total[:, :LANES] * keep(w))
@@ -578,14 +589,14 @@
             part = modes[b * per_node : (b + 1) * per_node]
             old.append(part[:, 2 * w * LANES : (2 * w + 1) * LANES])
             source.append(part[:, (2 * w + 1) * LANES : (2 * w + 2) * LANES] - stiff * old[-1])
-        divisor = 1.0 + STEP_HALF * stiff
+        inverse = table["inverse"].get(w * per_node, per_node)
         mid = sum(quad_weights[0][b] * source[b] for b in range(z.nodes))
-        mid = (mid + old[0] + STEP_HALF * stiff * old[1]) / divisor
+        mid = (mid + old[0] + STEP_HALF * stiff * old[1]) * inverse
         end = sum(quad_weights[1][b] * source[b] for b in range(z.nodes))
         end = end + mid + STEP_HALF * stiff * old[2]
         evals.append(old[1])
         evals.append(mid)
-        later.append((end, divisor))
+        later.append((end, inverse))
         old_of.append(old)
         mid_of.append(mid)
 
@@ -599,20 +610,25 @@
             ],
             0,
         ).astype(bf)
-        out = matmul_nt(left, legendre(w)[:, :LANES])
-        for s in range(slots):
-            for e in range(2):
-                at = (s * 2 + e) * per_node
-                coarse_s[e, pl.ds(w * slots + s, per_node, stride=z.coarse_columns), :] = out[at : at + per_node]
+        out = matmul_nt(left, legendre_s[w, :, :LANES])
+        coarse_s[w * slots * 2 * per_node : (w + 1) * slots * 2 * per_node, :] = out
 
     both_c = 2 * z.coarse_columns
     for a in range(z.levels):
-        pieces = [coarse_s[e, a * both_c : (a + 1) * both_c, :].astype(bf) for e in range(2)]
+        pieces = []
+        for e in range(2):
+            at = e * per_node + a * 2
+            piece = [
+                coarse_s[pl.ds(at + c, z.coarse_columns, stride=2 * per_node), :] for c in range(2)
+            ]
+            pieces.append(jnp.concatenate(piece, 0).astype(bf))
         grid = matmul(table["coarse_wave"].get(), jnp.concatenate(pieces, 1))
-        product = (grid * grid).astype(bf)
-        back = matmul(table["coarse_quad"].get(a * both_c, both_c), product)
+        coarse_product_s[a] = (grid * grid).astype(bf)
+    for a in range(z.levels):
+        back = matmul(table["coarse_quad"].get(a * both_c, both_c), coarse_product_s[a])
         for e in range(2):
-            coarse_back_s[e, a * both_c : (a + 1) * both_c, :] = back[:, e * LANES : (e + 1) * LANES]
+            values = back[:, e * LANES : (e + 1) * LANES] * gauss
+            coarse_back_s[e, a * both_c : (a + 1) * both_c, :] = values
 
     tends = []
     for w in range(z.n_wave):
@@ -624,7 +640,7 @@
             ],
             0,
         )
-        out = matmul(left, weighted(w)[:, :LANES])
+        out = matmul(left, legendre_s[w, :, :LANES])
         for e in range(2):
             total = None
             for s in range(slots):
@@ -636,8 +652,8 @@
     for w in range(z.n_wave):
         before = coarse_modes[:, 2 * w * LANES : (2 * w + 1) * LANES]
         fresh = coarse_modes[:, (2 * w + 1) * LANES : (2 * w + 2) * LANES]
-        end, divisor = later[w]
-        end = (end + STEP_HALF * (fresh - before)) / divisor
+        end, inverse = later[w]
+        end = (end + STEP_HALF * (fresh - before)) * inverse
         change_s[w, :per_node, :] = mid_of[w] - old_of[w][1]
         change_s[w, per_node:, :] = end - old_of[w][2]
 
@@ -738,17 +754,19 @@
         block, ("wave", "lev"), 0, 0, tiled=True, axis_index_groups=groups
     )
     fine_amp, coarse_amp = z.fine_width**-0.5, z.coarse**-0.5
-    basis = wave_rows(z.fine_width, longitudes, fine_amp)
+    order = np.arange(2 * z.fine_width).reshape(2, -1)
+    order = np.concatenate([order[:, : z.coarse].reshape(-1), order[:, z.coarse :].reshape(-1)])
+    basis = wave_rows(z.fine_width, longitudes, fine_amp)[order]
     spread = interpolation(z.points, longitudes, 2 * (z.fine_width - 1))
     spread *= 2.0 * z.fine_width / longitudes
     coarse_spread = interpolation(z.coarse_points, longitudes, 2 * (z.coarse - 1))
     coarse_spread *= 2.0 * z.coarse / (longitudes // 2) * (coarse_amp / fine_amp)
     coarse_spread[1::2] = 0.0
-    sampled = wave_rows(z.fine_width, z.points, fine_amp).T
+    sampled = wave_rows(z.fine_width, z.points, fine_amp)[order].T
     coarse_sampled = wave_rows(z.coarse, z.coarse_points, coarse_amp).T
     constants = [jnp.asarray(c, bf) for c in (basis, spread, coarse_spread, sampled, coarse_sampled)]
     layout, picks = mix_constants(z)
-    staged = [fold_pairs[None], grid_coef, *constants, jnp.stack([modes_from, modes_to]), picks]
+    staged = [fold_pairs[None], grid_coef, *constants, modes_from, modes_to, picks]
     wide = 2 * LANES
     (_, narrow_shape), (_, full_shape) = parts(z)
     tables = pl.pallas_call(
@@ -758,7 +776,6 @@
         out_specs=(vmem,) * 2,
         scratch_shapes=[
             pltpu.VMEM((z.levels * 2 * z.fine_width, longitudes), bf),
-            pltpu.VMEM((z.levels * 2 * z.coarse, longitudes), bf),
             pltpu.SemaphoreType.DMA((len(staged),)),
         ]
         + [pltpu.VMEM(array.shape, array.dtype) for array in staged],
@@ -784,12 +801,15 @@
             pltpu.VMEM((z.rows * z.fine_columns, lat_rows), f32),
             pltpu.VMEM((z.rows * z.fine_columns, lat_rows), f32),
             pltpu.VMEM((z.n_wave, z.rows + SUBLANES, wide), f32),
-            pltpu.VMEM((2, z.per_node * z.coarse_columns, lat_rows), f32),
+            pltpu.VMEM((2 * z.per_node * z.coarse_columns, lat_rows), f32),
             pltpu.VMEM((2, z.per_node * z.coarse_columns, lat_rows), f32),
             pltpu.VMEM((z.n_wave, (z.nodes - 1) * z.per_node, LANES), f32),
             pltpu.VMEM(narrow_shape, bf),
             pltpu.VMEM(full_shape, f32),
             pltpu.SemaphoreType.DMA((2,)),
+            pltpu.VMEM((z.n_wave, lat_rows, wide), bf),
+            pltpu.VMEM((z.levels, z.points, z.nodes * LANES), bf),
+            pltpu.VMEM((z.levels, z.coarse_points, 2 * LANES), bf),
         ],
         compiler_params=pltpu.CompilerParams(vmem_limit_bytes=VMEM_BYTES),
         name="sweep",

time: 27.9 us -> 26.1 us (0.935)
  Pallas kernels: 14.9 us -> 13.2 us
  other arithmetic: 1.31 us -> 0 us
  waiting for transfers between devices: 2.26 us -> 3.5 us
    pallas_call x1, Pallas kernels: 6.79 us -> 5.01 us  [replicated_plan(): pl.pallas_call(functools.partial(sweep_kernel, z), out_shape=(shape((z.le...]
    another operation x1 -> x0, other arithmetic: 1.31 us -> none  [replicated_plan(): jnp.stack([modes_from, modes_to])]
    all_to_all x1, waiting for transfers between devices: 0.82 us -> 2.06 us  [replicated_plan(): lax.all_to_all(block, ('wave', 'lev'), 0, 0, tiled=True, axis_index_group...]
  transfers between devices with their start and end apart: 2 -> 2, of which waited for: 2 -> 2; matrix products, arithmetic and copies ran while one was open for 5% -> 0% of each run, Pallas kernels for 24% -> 26%
where the time goes in v1:
time: 26.1 us; the launch traced here: 25.7 us
  Pallas kernels  13.2 us (51%)
  starting transfers between devices  8.36 us (32%)
  waiting for transfers between devices  3.5 us (13%)
  between operations  0.66 us (3%)
    all_to_all x1, starting transfers between devices, replicated_plan(): lax.all_to_all(block, ('wave', 'lev'), 0, 0, tiled=True, axis_index_group...  8.35 us
    pallas_call x1, Pallas kernels, replicated_plan(): pl.pallas_call(functools.partial(tables_kernel, z, layout), out_shape=(sh...  6.56 us
    pallas_call x1, Pallas kernels, replicated_plan(): pl.pallas_call(functools.partial(sweep_kernel, z), out_shape=(shape((z.le...  5.01 us
    all_to_all x1, waiting for transfers between devices, replicated_plan(): lax.all_to_all(block, ('wave', 'lev'), 0, 0, tiled=True, axis_index_group...  2.06 us
    pallas_call x1, Pallas kernels, replicated_plan(): pl.pallas_call(functools.partial(pack_kernel, z), out_shape=shape((z.chip...  1.64 us
    ppermute x1, waiting for transfers between devices, replicated_plan(): lax.ppermute(own, ('wave', 'lev'), [(i, i ^ 1) for i in range(2 * z.chips)])  1.44 us
  transfers between devices with their start and end apart: 2, of which 2 were waited for; matrix products, arithmetic and copies ran while one was open for 0% of the time, Pallas kernels for 26%

profile of v1, /device:TPU:0, one launch (start us, length us, event | category | flops | bytes accessed | tf_op | source)
XLA Modules:
  0.0 25.7 jit_solution(5111309073586705199)
XLA Ops:
  0.6 1.6 %pack.1 = bf16[16,48,128]{2,1,0:T(8,128)(2,1)} custom-call(f32[2,3,3,2,49]{4,3,2,1,0:T(2,128)} %bitcast.5, bf16[3,24,49]{2,1,0:T(8,128)(2,1)} %leg_hbm.1, f32[1,24]{1,0:T(1,128)} %bitcast.7), custom_call_target="tpu_custom_call" | custom-call | tf_op jit(solution)/shard_map/pack/pallas_call | solution.py:738
  2.3 8.4 %all-to-all-start = ((bf16[16,48,128]{2,1,0:T(8,128)(2,1)}), bf16[16,48,128]{2,1,0:T(8,128)(2,1)S(1)}, u32[]{:S(2)}, u32[]{:S(2)}) async-start(bf16[16,48,128]{2,1,0:T(8,128)(2,1)} %pack.1), calls=%async_computation | async-start | bytes 393216 | tf_op jit(solution)/shard_map/all_to_all | solution.py:753
  10.6 0.0 copy-start
  10.6 6.6 %tables.1 = (bf16[1536,192]{1,0:T(8,128)(2,1)}, f32[336,256]{1,0:T(8,128)}) custom-call(f32[8]{0:T(128)} %rate_ref.1, s32[24]{0:T(128)} %fold_smem.1, s32[1,24]{1,0:T(1,128)} %bitcast.10, f32[8,2560]{1,0:T(8,128)} %refs_1_.1, bf16[96,2560]{1,0:T(8,128)(2,1)} %constant.12.clone.refs_2_, bf16[2560,192]{1,0:T(8,128)(2,1)} %constant.13.clone.refs_3_, ...), custom_call_target="tpu_custom_call" | custom-call | flops 1000000000 | bytes 4000000 | tf_op jit(solution)/shard_map/tables/pallas_call | solution.py:772
  17.2 2.1 %all-to-all-done.own_ref = bf16[16,48,128]{2,1,0:T(8,128)(2,1)S(1)} async-done(((bf16[16,48,128]{2,1,0:T(8,128)(2,1)}), bf16[16,48,128]{2,1,0:T(8,128)(2,1)S(1)}, u32[]{:S(2)}, u32[]{:S(2)}) %all-to-all-start) | async-done | bytes 196640 | tf_op jit(solution)/shard_map/all_to_all | solution.py:753
  19.3 0.0 collective-permute-start
  19.3 1.4 %collective-permute-done.other_ref = bf16[16,48,128]{2,1,0:T(8,128)(2,1)S(1)} collective-permute-done((bf16[16,48,128]{2,1,0:T(8,128)(2,1)S(1)}, bf16[16,48,128]{2,1,0:T(8,128)(2,1)S(1)}, u32[]{:S(2)}, u32[]{:S(2)}) %collective-permute-start) | collective-permute-done | bytes 196640 | tf_op jit(solution)/shard_map/ppermute | solution.py:787
  20.7 0.0 copy-done
  20.7 5.0 %sweep.1 = (f32[2,2,3,2,49]{4,3,2,1,0:T(2,128)}, f32[2,3,3,2,49]{4,3,2,1,0:T(2,128)}) custom-call(bf16[16,48,128]{2,1,0:T(8,128)(2,1)S(1)} %all-to-all-done.own_ref, bf16[16,48,128]{2,1,0:T(8,128)(2,1)S(1)} %collective-permute-done.other_ref, f32[2,3,3,2,49]{4,3,2,1,0:T(2,128)S(1)} %bitcast.6, bf16[1536,192]{1,0:T(8,128)(2,1)} %get-tuple-element.12.narrow_hbm, ...), custom_call_target="tpu_custom_call" | custom-call | tf_op jit(solution)/shard_map/sweep/pallas_call | solution.py:790
Async XLA Ops:
  2.3 17.0 %all-to-all-start = ((bf16[16,48,128]{2,1,0:T(8,128)(2,1)}), bf16[16,48,128]{2,1,0:T(8,128)(2,1)S(1)}, u32[]{:S(2)}, u32[]{:S(2)}) async-start(bf16[16,48,128]{2,1,0:T(8,128)(2,1)} %pack.1), calls=%async_computation | async-start | bytes 393216 | tf_op jit(solution)/shard_map/all_to_all | solution.py:753
  10.6 10.1 %copy-start = (f32[2,3,2,3,49]{4,2,3,1,0:T(2,128)S(1)}, f32[2,3,2,3,49]{4,2,3,1,0:T(2,128)}, u32[]{:S(2)}) copy-start(f32[2,3,2,3,49]{4,2,3,1,0:T(2,128)} %param.14) | copy-start | bytes 21172
  19.3 1.4 %collective-permute-start = (bf16[16,48,128]{2,1,0:T(8,128)(2,1)S(1)}, bf16[16,48,128]{2,1,0:T(8,128)(2,1)S(1)}, u32[]{:S(2)}, u32[]{:S(2)}) collective-permute-start(bf16[16,48,128]{2,1,0:T(8,128)(2,1)S(1)} %all-to-all-done.own_ref), channel_id=1, source_target_pairs={{0,1},{1,0},{2,3},{3,2},{4,5},{5,4},{6,7},{7,6},{8,9},{9,8},{10,11... | collective-permute-start | bytes 589832 | tf_op jit(solution)/shard_map/ppermute | solution.py:787

commit v2 on v1

--- a/solution.py
+++ b/solution.py
@@ -236,6 +236,7 @@
         self.fine_width = self.fine_rows - 1
         self.coarse = self.fine_width // 2
         self.levels = self.n_lev * self.lev_dev
+        self.own_levels = self.n_pair * self.lev_dev
         self.dev_rows = self.lev_dev * self.nodes * 2
         self.rows = self.levels * self.nodes * 2
         self.per_node = self.levels * 2
@@ -247,6 +248,9 @@
         self.unit = LANES // self.groups
         self.block_rows = self.lats + SUBLANES + self.state_rows
         self.chips = self.n_wave * self.n_pair
+        lead = self.chips // 2 - 1
+        self.order = [lead] + [i for i in range(self.chips) if i != lead]
+        self.position = [self.order.index(i) for i in range(self.chips)]
         self.fine_columns = self.n_wave * self.slots * 2
         self.coarse_columns = self.n_wave * self.slots
         self.points = round_up(4 * (self.fine_width - 1) + 1, 32)
@@ -256,9 +260,7 @@
 def parts(z):
     narrow = dict(
         wave=(z.points, 2 * z.fine_columns),
-        quad=(z.levels * 2 * z.fine_columns, z.points),
         coarse_wave=(z.coarse_points, 2 * z.coarse_columns),
-        coarse_quad=(z.levels * 2 * z.coarse_columns, z.coarse_points),
         mix_to=(z.rows, 3 * z.rows),
         mix_from=(z.per_node, 3 * z.per_node),
         mix_back=(z.per_node, 3 * z.per_node),
@@ -279,7 +281,11 @@
             at += round_up(count, unit)
         return out, (at, max(columns for _, columns in shapes.values()))
 
-    return placed(narrow, 2 * SUBLANES), placed(full, SUBLANES)
+    quads = dict(
+        quad=(z.own_levels * 2 * z.fine_columns, z.points),
+        coarse_quad=(z.own_levels * 2 * z.coarse_columns, z.coarse_points),
+    )
+    return [placed(shapes, 2 * SUBLANES) for shapes in (narrow, full, quads)]
 
 
 class Table:
@@ -295,10 +301,11 @@
         self.ref[begin : begin + values.shape[0], : self.columns] = values
 
 
-def named(z, narrow_ref, full_ref):
-    (narrow, _), (full, _) = parts(z)
-    tables = {name: Table(narrow_ref, place) for name, place in narrow.items()}
-    return tables | {name: Table(full_ref, place) for name, place in full.items()}
+def named(z, *refs):
+    tables = {}
+    for ref, (places, _) in zip(refs, parts(z)):
+        tables |= {name: Table(ref, place) for name, place in places.items()}
+    return tables
 
 
 def copies_in(sources, targets, sems):
@@ -357,15 +364,16 @@
         out_ref[i] = block
 
 
-def mix_matrix(pick_left, matrix, pick_right, mask, cut):
-    values = matmul_exact(matmul_exact(pick_left, matrix), pick_right) * mask
-    high, low = high_low(values)
-    lane = lax.broadcasted_iota(jnp.int32, values.shape, 1)
-    return jnp.where(lane < cut, high.astype(jnp.float32), low.astype(jnp.float32)).astype(jnp.bfloat16)
+def mix_matrix(pick_left, matrix, pick_right, mask):
+    bf, f32 = jnp.bfloat16, jnp.float32
+    high, low = high_low(matrix)
+    left = pick_left.astype(bf)
+    halves = jnp.concatenate([matmul(left, high).astype(bf), matmul(left, low).astype(bf)], 1)
+    return (matmul(halves, pick_right.astype(bf)) * mask.astype(f32)).astype(bf)
 
 
 def tables_kernel(z, layout, rate_ref, fold_smem, *refs):
-    inputs, outputs, scratch = refs[:10], refs[10:12], refs[12:]
+    inputs, outputs, scratch = refs[:10], refs[10:13], refs[13:]
     (scaled_s, sems), staged = scratch[:2], scratch[2:]
     copies = copies_in(inputs, staged, sems)
     fold_ref, coef_ref, basis_ref, spread_ref, coarse_spread_ref = staged[:5]
@@ -376,70 +384,6 @@
     core = lax.rem(lev, 2)
     waves, coarse = z.fine_width, z.coarse
     half = z.fine_columns
-
-    for copy in copies[:3]:
-        copy.wait()
-
-    def wave_column(count, per_slot):
-        row = lax.broadcasted_iota(jnp.int32, (count, z.coarse_columns), 0)
-        lane = lax.broadcasted_iota(jnp.int32, (count, z.coarse_columns), 1)
-        inside = (row >= lane * per_slot) & (row < (lane + 1) * per_slot)
-        small = jnp.sum(jnp.where(inside, fold_ref[...].astype(f32), 0.0), axis=1, keepdims=True)
-        if per_slot == 1:
-            return small
-        first = lax.broadcasted_iota(jnp.int32, (count, 1), 0) & 1
-        return jnp.where(first == 0, small, waves - 1 - small)
-
-    def one_hot(count, per_slot, width):
-        column = wave_column(count, per_slot)
-        lane = lax.broadcasted_iota(jnp.int32, (count, 2 * width), 1).astype(f32)
-        extra = width - coarse
-        top = lane == jnp.where(column < coarse, column, column + coarse)
-        bottom = lane == jnp.where(column < coarse, column + coarse, column + coarse + extra)
-        return jnp.concatenate([top.astype(f32), bottom.astype(f32)], 0).astype(bf)
-
-    hot = one_hot(half, 2, waves)
-    coarse_hot = one_hot(z.coarse_columns, 1, coarse)
-    short, long = 2 * coarse, 2 * (waves - coarse)
-    levels = [
-        (2 * x + (core if o == 0 else 1 - core)) * z.lev_dev + al
-        for x in range(z.n_pair)
-        for o in range(2)
-        for al in range(z.lev_dev)
-    ]
-    chunk = 2 * LANES
-    for begin in range(0, basis_ref.shape[1], chunk):
-        values = basis_ref[:, begin : begin + chunk].astype(f32)
-        for a, level in enumerate(levels):
-            scaled = coef_ref[pl.ds(level, 1), begin : begin + chunk] * values
-            scaled_s[a * short : (a + 1) * short, begin : begin + chunk] = scaled[:short].astype(bf)
-            at = z.levels * short + a * long
-            scaled_s[at : at + long, begin : begin + chunk] = scaled[short:].astype(bf)
-    for copy in copies[3:]:
-        copy.wait()
-    out["wave"].put(matmul_nt(sampled_ref[...], hot).astype(bf))
-    out["coarse_wave"].put(matmul_nt(coarse_sampled_ref[...], coarse_hot).astype(bf))
-    coarse_quad = matmul(scaled_s[: z.levels * short, :], coarse_spread_ref[...]).astype(bf)
-    quad = matmul(scaled_s[...], spread_ref[...]).astype(bf)
-    for a in range(z.levels):
-        at = z.levels * short + a * long
-        pair = jnp.concatenate([quad[a * short : (a + 1) * short], quad[at : at + long]], 0)
-        values = matmul(hot, pair).astype(bf)
-        out["quad"].put(values, a * values.shape[0])
-        values = matmul(coarse_hot, coarse_quad[a * short : (a + 1) * short]).astype(bf)
-        out["coarse_quad"].put(values, a * values.shape[0])
-
-    def pick(name, index=0):
-        at, rows, columns = layout[name]
-        return picks_ref[pl.ds(pl.multiple_of(at + index * rows, SUBLANES), rows), :columns]
-
-    def mix(left, matrix, right, mask):
-        return mix_matrix(left, matrix[...], right, mask, right.shape[1] // 3 * 2)
-
-    out["mix_to"].put(mix(pick("to_left"), to_ref, pick("to_right", core), pick("to_mask")))
-    out["mix_from"].put(mix(pick("from_left", core), from_ref, pick("from_right"), pick("from_mask")))
-    out["mix_back"].put(mix(pick("back_left"), to_ref, pick("back_right", core), pick("from_mask")))
-    out["lift"].put(mix(pick("lift_left", lev), from_ref, pick("lift_right"), pick("lift_mask")))
 
     wide = 2 * LANES
     lane = lax.broadcasted_iota(jnp.int32, (1, wide), 1)
@@ -472,6 +416,65 @@
         out["stiff"].put(stiff, w * z.per_node)
         out["inverse"].put(1.0 / (1.0 + STEP_HALF * stiff), w * z.per_node)
 
+    for copy in copies[:3]:
+        copy.wait()
+
+    def wave_column(count, per_slot):
+        row = lax.broadcasted_iota(jnp.int32, (count, z.coarse_columns), 0)
+        lane = lax.broadcasted_iota(jnp.int32, (count, z.coarse_columns), 1)
+        inside = (row >= lane * per_slot) & (row < (lane + 1) * per_slot)
+        small = jnp.sum(jnp.where(inside, fold_ref[...].astype(f32), 0.0), axis=1, keepdims=True)
+        if per_slot == 1:
+            return small
+        first = lax.broadcasted_iota(jnp.int32, (count, 1), 0) & 1
+        return jnp.where(first == 0, small, waves - 1 - small)
+
+    def one_hot(count, per_slot, width):
+        column = wave_column(count, per_slot)
+        lane = lax.broadcasted_iota(jnp.int32, (count, 2 * width), 1).astype(f32)
+        extra = width - coarse
+        top = lane == jnp.where(column < coarse, column, column + coarse)
+        bottom = lane == jnp.where(column < coarse, column + coarse, column + coarse + extra)
+        return jnp.concatenate([top.astype(f32), bottom.astype(f32)], 0).astype(bf)
+
+    hot = one_hot(half, 2, waves)
+    coarse_hot = one_hot(z.coarse_columns, 1, coarse)
+    short, long = 2 * coarse, 2 * (waves - coarse)
+    levels = [(2 * x + core) * z.lev_dev + al for x in range(z.n_pair) for al in range(z.lev_dev)]
+    chunk = 2 * LANES
+    for begin in range(0, basis_ref.shape[1], chunk):
+        values = basis_ref[:, begin : begin + chunk].astype(f32)
+        for a, level in enumerate(levels):
+            scaled = coef_ref[pl.ds(level, 1), begin : begin + chunk] * values
+            scaled_s[a * short : (a + 1) * short, begin : begin + chunk] = scaled[:short].astype(bf)
+            at = z.own_levels * short + a * long
+            scaled_s[at : at + long, begin : begin + chunk] = scaled[short:].astype(bf)
+    for copy in copies[3:]:
+        copy.wait()
+    out["wave"].put(matmul_nt(sampled_ref[...], hot).astype(bf))
+    out["coarse_wave"].put(matmul_nt(coarse_sampled_ref[...], coarse_hot).astype(bf))
+    coarse_quad = matmul(scaled_s[: z.own_levels * short, :], coarse_spread_ref[...]).astype(bf)
+    quad = matmul(scaled_s[...], spread_ref[...]).astype(bf)
+    for a in range(z.own_levels):
+        at = z.own_levels * short + a * long
+        pair = jnp.concatenate([quad[a * short : (a + 1) * short], quad[at : at + long]], 0)
+        values = matmul(hot, pair).astype(bf)
+        out["quad"].put(values, a * values.shape[0])
+        values = matmul(coarse_hot, coarse_quad[a * short : (a + 1) * short]).astype(bf)
+        out["coarse_quad"].put(values, a * values.shape[0])
+
+    def pick(name, index=0):
+        at, rows, columns = layout[name]
+        return picks_ref[pl.ds(pl.multiple_of(at + index * rows, SUBLANES), rows), :columns]
+
+    def mix(left, matrix, right, mask):
+        return mix_matrix(left, matrix[...], right, mask)
+
+    out["mix_to"].put(mix(pick("to_left"), to_ref, pick("to_right", core), pick("to_mask")))
+    out["mix_from"].put(mix(pick("from_left", core), from_ref, pick("from_right"), pick("from_mask")))
+    out["mix_back"].put(mix(pick("back_left"), to_ref, pick("back_right", core), pick("from_mask")))
+    out["lift"].put(mix(pick("lift_left", lev), from_ref, pick("lift_right"), pick("lift_mask")))
+
 
 def sweep_kernel(
     z,
@@ -480,6 +483,8 @@
     state_ref,
     narrow_hbm,
     full_hbm,
+    quads_hbm,
+    other_quads_hbm,
     corrected_ref,
     tend_ref,
     leg_s,
@@ -492,6 +497,8 @@
     change_s,
     narrow_ref,
     full_ref,
+    quads_ref,
+    other_quads_ref,
     sems,
     legendre_s,
     product_s,
@@ -500,7 +507,17 @@
     bf, f32 = jnp.bfloat16, jnp.float32
     slots, rows, lats, per_node = z.slots, z.rows, z.lats, z.per_node
     table = named(z, narrow_ref, full_ref)
-    copies = copies_in((full_hbm, narrow_hbm), (full_ref, narrow_ref), sems)
+    quads = [named(z, *[ref] * 3) for ref in (quads_ref, other_quads_ref)]
+    copies = copies_in(
+        (full_hbm, narrow_hbm, quads_hbm, other_quads_hbm),
+        (full_ref, narrow_ref, quads_ref, other_quads_ref),
+        sems,
+    )
+
+    def quad(name, a, count):
+        lev, inner = a // z.lev_dev, a % z.lev_dev
+        return quads[lev % 2][name].get((lev // 2 * z.lev_dev + inner) * count, count)
+
     wide = 2 * LANES
     all_lats = z.n_lev * lats
 
@@ -517,7 +534,7 @@
         for x in range(z.n_pair):
             for o, ref in enumerate((own_ref, other_ref)):
                 d = 2 * x + o
-                block = ref[w * z.n_pair + x].astype(f32)
+                block = ref[z.position[w * z.n_pair + x]].astype(f32)
                 extra = block[lats : lats + SUBLANES]
                 leg_s[w, d * lats : (d + 1) * lats, :LANES] = block[:lats]
                 state_at = d * z.dev_rows
@@ -546,7 +563,8 @@
         left = jnp.concatenate([state * member(w, j) for j in range(2 * slots)], 0).astype(bf)
         fourier_s[w * 2 * slots * rows : (w + 1) * 2 * slots * rows, :] = matmul_nt(left, legendre_s[w])
 
-    copies[1].wait()
+    for copy in copies[1:]:
+        copy.wait()
     both = 2 * z.fine_columns
     half = z.fine_columns
     for a in range(z.levels):
@@ -558,7 +576,7 @@
         grid = matmul(table["wave"].get(), jnp.concatenate(pieces, 1))
         product_s[a] = (grid * grid).astype(bf)
     for a in range(z.levels):
-        back = matmul(table["quad"].get(a * both, both), product_s[a])
+        back = matmul(quad("quad", a, both), product_s[a])
         for b in range(z.nodes):
             values = back[:, b * LANES : (b + 1) * LANES] * gauss
             back_s[(a * z.nodes + b) * both : (a * z.nodes + b + 1) * both, :] = values
@@ -625,7 +643,7 @@
         grid = matmul(table["coarse_wave"].get(), jnp.concatenate(pieces, 1))
         coarse_product_s[a] = (grid * grid).astype(bf)
     for a in range(z.levels):
-        back = matmul(table["coarse_quad"].get(a * both_c, both_c), coarse_product_s[a])
+        back = matmul(quad("coarse_quad", a, both_c), coarse_product_s[a])
         for e in range(2):
             values = back[:, e * LANES : (e + 1) * LANES] * gauss
             coarse_back_s[e, a * both_c : (a + 1) * both_c, :] = values
@@ -691,6 +709,12 @@
     def thrice(matrix):
         return np.concatenate([matrix] * 3, -1)
 
+    def halves(matrix):
+        zero = np.zeros_like(matrix)
+        return np.concatenate(
+            [np.concatenate([matrix, matrix, zero], 1), np.concatenate([zero, zero, matrix], 1)]
+        )
+
     rb, rq, rc = grid(node, level, part)
     ca, cb, cc = grid(level, node, part)
     sa, sc = grid(level, part)
@@ -702,15 +726,15 @@
     by_core = range(2)
     constants = dict(
         to_left=[pick(rq)],
-        to_right=[thrice(pick(ordered(ca, k)).T) for k in by_core],
+        to_right=[halves(pick(ordered(ca, k)).T) for k in by_core],
         to_mask=[thrice(to_mask)],
         from_left=[pick(ordered(sa, k)) for k in by_core],
-        from_right=[thrice(pick(sa).T)],
+        from_right=[halves(pick(sa).T)],
         from_mask=[thrice(same_part)],
         back_left=[pick(sa)],
-        back_right=[thrice(pick(ordered(sa, k)).T) for k in by_core],
+        back_right=[halves(pick(ordered(sa, k)).T) for k in by_core],
         lift_left=[pick(k * z.lev_dev + la) for k in range(z.n_lev)],
-        lift_right=[thrice(pick(kq).T)],
+        lift_right=[halves(pick(kq).T)],
         lift_mask=[thrice(lift_mask)],
     )
     wide = max(m[0].shape[1] for m in constants.values())
@@ -749,7 +773,7 @@
         ],
         name="pack",
     )(stored, legendre, gauss_weights[None])
-    groups = [[2 * i + c for i in range(z.chips)] for c in range(2)]
+    groups = [[2 * i + c for i in z.order] for c in range(2)]
     own = lax.all_to_all(
         block, ("wave", "lev"), 0, 0, tiled=True, axis_index_groups=groups
     )
@@ -768,14 +792,14 @@
     layout, picks = mix_constants(z)
     staged = [fold_pairs[None], grid_coef, *constants, modes_from, modes_to, picks]
     wide = 2 * LANES
-    (_, narrow_shape), (_, full_shape) = parts(z)
-    tables = pl.pallas_call(
+    narrow_shape, full_shape, quads_shape = [entry[1] for entry in parts(z)]
+    narrow, full, quads = pl.pallas_call(
         functools.partial(tables_kernel, z, layout),
-        out_shape=(shape(narrow_shape, bf), shape(full_shape, f32)),
+        out_shape=(shape(narrow_shape, bf), shape(full_shape, f32), shape(quads_shape, bf)),
         in_specs=[smem, smem] + [hbm] * len(staged),
-        out_specs=(vmem,) * 2,
+        out_specs=(vmem,) * 3,
         scratch_shapes=[
-            pltpu.VMEM((z.levels * 2 * z.fine_width, longitudes), bf),
+            pltpu.VMEM((z.own_levels * 2 * z.fine_width, longitudes), bf),
             pltpu.SemaphoreType.DMA((len(staged),)),
         ]
         + [pltpu.VMEM(array.shape, array.dtype) for array in staged],
@@ -783,8 +807,10 @@
         name="tables",
     )(mode_rates, fold_pairs, *staged)
 
-    own, *tables = lax.optimization_barrier((own, *tables))
-    other = lax.ppermute(own, ("wave", "lev"), [(i, i ^ 1) for i in range(2 * z.chips)])
+    partners = [(i, i ^ 1) for i in range(2 * z.chips)]
+    other_quads = lax.ppermute(quads, ("wave", "lev"), partners)
+    own, narrow = lax.optimization_barrier((own, narrow))
+    other = lax.ppermute(own, ("wave", "lev"), partners)
 
     lat_rows = round_up(z.n_lev * z.lats, LANES)
     corrected, fine_tend = pl.pallas_call(
@@ -793,7 +819,7 @@
             shape((z.lev_dev, z.nodes - 1, z.slots, 2, z.fine_rows), f32),
             shape(stored.shape, f32),
         ),
-        in_specs=[vmem] * 3 + [hbm] * 2,
+        in_specs=[vmem] * 3 + [hbm] * 4,
         out_specs=(vmem, vmem),
         scratch_shapes=[
             pltpu.VMEM((z.n_wave, lat_rows, wide), f32),
@@ -806,14 +832,16 @@
             pltpu.VMEM((z.n_wave, (z.nodes - 1) * z.per_node, LANES), f32),
             pltpu.VMEM(narrow_shape, bf),
             pltpu.VMEM(full_shape, f32),
-            pltpu.SemaphoreType.DMA((2,)),
+            pltpu.VMEM(quads_shape, bf),
+            pltpu.VMEM(quads_shape, bf),
+            pltpu.SemaphoreType.DMA((4,)),
             pltpu.VMEM((z.n_wave, lat_rows, wide), bf),
             pltpu.VMEM((z.levels, z.points, z.nodes * LANES), bf),
             pltpu.VMEM((z.levels, z.coarse_points, 2 * LANES), bf),
         ],
         compiler_params=pltpu.CompilerParams(vmem_limit_bytes=VMEM_BYTES),
         name="sweep",
-    )(own, other, stored, *tables)
+    )(own, other, stored, narrow, full, quads, other_quads)
     return (jnp.swapaxes(corrected, 2, 3), jnp.swapaxes(fine_tend, 2, 3))
 
 

time: 26.1 us -> 24.4 us (0.935)
  waiting for transfers between devices: 3.5 us -> 2.01 us
  Pallas kernels: 13.2 us -> 12 us
  starting transfers between devices: 8.36 us -> 8.94 us
  local copies, waits for them, and re-layouts: 0.01 us -> 0.44 us
    all_to_all x1, waiting for transfers between devices: 2.06 us -> 0.46 us  [replicated_plan(): lax.all_to_all(block, ('wave', 'lev'), 0, 0, tiled=True, axis_index_group...]
    pallas_call x1, Pallas kernels: 6.56 us -> 5.31 us  [replicated_plan(): pl.pallas_call(functools.partial(tables_kernel, z, layout), out_shape=(sh...]
    all_to_all x1, starting transfers between devices: 8.35 us -> 8.82 us  [replicated_plan(): lax.all_to_all(block, ('wave', 'lev'), 0, 0, tiled=True, axis_index_group...]
    unnamed x2 -> x4, local copies, waits for them, and re-layouts: 0.01 us -> 0.44 us
    ppermute x1 -> x2, waiting for transfers between devices: 1.44 us -> 1.56 us  [the longest x1 1.28 us: replicated_plan(): other_quads = lax.ppermute(quads, ('wave', 'lev'), partners)]
  transfers between devices with their start and end apart: 2 -> 3, of which waited for: 2 -> 3; matrix products, arithmetic and copies ran while one was open for 0% -> 0% of each run, Pallas kernels for 26% -> 22%
where the time goes in v2:
time: 24.4 us; the launch traced here: 24 us
  Pallas kernels  12 us (49%)
  starting transfers between devices  8.94 us (37%)
  waiting for transfers between devices  2.01 us (8%)
  between operations  0.66 us (3%)
  local copies, waits for them, and re-layouts  0.44 us (2%)
    all_to_all x1, starting transfers between devices, replicated_plan(): lax.all_to_all(block, ('wave', 'lev'), 0, 0, tiled=True, axis_index_group...  8.82 us
    pallas_call x1, Pallas kernels, replicated_plan(): pl.pallas_call(functools.partial(tables_kernel, z, layout), out_shape=(sh...  5.31 us
    pallas_call x1, Pallas kernels, replicated_plan(): pl.pallas_call(functools.partial(sweep_kernel, z), out_shape=(shape((z.le...  5.03 us
    pallas_call x1, Pallas kernels, replicated_plan(): pl.pallas_call(functools.partial(pack_kernel, z), out_shape=shape((z.chip...  1.63 us
    ppermute x1, waiting for transfers between devices, replicated_plan(): other_quads = lax.ppermute(quads, ('wave', 'lev'), partners)  1.28 us
  transfers between devices with their start and end apart: 3, of which 3 were waited for; matrix products, arithmetic and copies ran while one was open for 0% of the time, Pallas kernels for 22%

profile of v2, /device:TPU:0, one launch (start us, length us, event | category | flops | bytes accessed | tf_op | source)
XLA Modules:
  0.0 24.0 jit_solution(6197052087897555773)
XLA Ops:
  0.6 1.6 %pack.1 = bf16[16,48,128]{2,1,0:T(8,128)(2,1)} custom-call(f32[2,3,3,2,49]{4,3,2,1,0:T(2,128)} %bitcast.5, bf16[3,24,49]{2,1,0:T(8,128)(2,1)} %leg_hbm.1, f32[1,24]{1,0:T(1,128)} %bitcast.7), custom_call_target="tpu_custom_call" | custom-call | tf_op jit(solution)/shard_map/pack/pallas_call | solution.py:762
  2.3 8.8 %all-to-all-start = ((bf16[16,48,128]{2,1,0:T(8,128)(2,1)}), bf16[16,48,128]{2,1,0:T(8,128)(2,1)S(1)}, u32[]{:S(2)}, u32[]{:S(2)}) async-start(bf16[16,48,128]{2,1,0:T(8,128)(2,1)} %pack.1), calls=%async_computation | async-start | bytes 393216 | tf_op jit(solution)/shard_map/all_to_all | solution.py:777
  11.1 0.0 copy-start
  11.1 5.3 %tables.1 = (bf16[384,144]{1,0:T(8,128)(2,1)}, f32[352,256]{1,0:T(8,128)}, bf16[576,192]{1,0:T(8,128)(2,1)}) custom-call(f32[8]{0:T(128)} %rate_ref.1, s32[24]{0:T(128)} %fold_smem.1, s32[1,24]{1,0:T(1,128)} %bitcast.10, f32[8,2560]{1,0:T(8,128)} %refs_1_.1, bf16[96,2560]{1,0:T(8,128)(2,1)} %constant.12.clone.refs_2_, ...), custom_call_target="tpu_custom_call" | custom-call | flops 1000000000 | bytes 4000000 | tf_op jit(solution)/shard_map/tables/pallas_call | solution.py:796
  16.4 0.1 collective-permute-start.1
  16.5 0.5 %all-to-all-done.own_ref = bf16[16,48,128]{2,1,0:T(8,128)(2,1)S(1)} async-done(((bf16[16,48,128]{2,1,0:T(8,128)(2,1)}), bf16[16,48,128]{2,1,0:T(8,128)(2,1)S(1)}, u32[]{:S(2)}, u32[]{:S(2)}) %all-to-all-start) | async-done | bytes 196640 | tf_op jit(solution)/shard_map/all_to_all | solution.py:777
  16.9 0.0 collective-permute-start
  17.0 1.3 %collective-permute-done.1.other_quads_hbm = bf16[576,192]{1,0:T(8,128)(2,1)S(1)} collective-permute-done((bf16[576,192]{1,0:T(8,128)(2,1)}, bf16[576,192]{1,0:T(8,128)(2,1)S(1)}, u32[]{:S(2)}, u32[]{:S(2)}) %collective-permute-start.1) | collective-permute-done | bytes 221216 | tf_op jit(solution)/shard_map/ppermute | solution.py:811
  18.3 0.0 copy-start.1
  18.3 0.3 %collective-permute-done.other_ref = bf16[16,48,128]{2,1,0:T(8,128)(2,1)S(1)} collective-permute-done((bf16[16,48,128]{2,1,0:T(8,128)(2,1)S(1)}, bf16[16,48,128]{2,1,0:T(8,128)(2,1)S(1)}, u32[]{:S(2)}, u32[]{:S(2)}) %collective-permute-start) | collective-permute-done | bytes 196640 | tf_op jit(solution)/shard_map/ppermute | solution.py:813
  18.5 0.4 %copy-done.1 = bf16[576,192]{1,0:T(8,128)(2,1)} copy-done((bf16[576,192]{1,0:T(8,128)(2,1)}, bf16[576,192]{1,0:T(8,128)(2,1)S(1)}, u32[]{:S(2)}) %copy-start.1) | copy-done | bytes 221208
  19.0 0.0 copy-done
  19.0 5.0 %sweep.1 = (f32[2,2,3,2,49]{4,3,2,1,0:T(2,128)}, f32[2,3,3,2,49]{4,3,2,1,0:T(2,128)}) custom-call(bf16[16,48,128]{2,1,0:T(8,128)(2,1)S(1)} %all-to-all-done.own_ref, bf16[16,48,128]{2,1,0:T(8,128)(2,1)S(1)} %collective-permute-done.other_ref, f32[2,3,3,2,49]{4,3,2,1,0:T(2,128)S(1)} %bitcast.6, bf16[384,144]{1,0:T(8,128)(2,1)} %get-tuple-element.11.narrow_hbm, ...), custom_call_target="tpu_custom_call" | custom-call | tf_op jit(solution)/shard_map/sweep/pallas_call | solution.py:816
Async XLA Ops:
  2.3 14.7 %all-to-all-start = ((bf16[16,48,128]{2,1,0:T(8,128)(2,1)}), bf16[16,48,128]{2,1,0:T(8,128)(2,1)S(1)}, u32[]{:S(2)}, u32[]{:S(2)}) async-start(bf16[16,48,128]{2,1,0:T(8,128)(2,1)} %pack.1), calls=%async_computation | async-start | bytes 393216 | tf_op jit(solution)/shard_map/all_to_all | solution.py:777
  11.1 7.9 %copy-start = (f32[2,3,2,3,49]{4,2,3,1,0:T(2,128)S(1)}, f32[2,3,2,3,49]{4,2,3,1,0:T(2,128)}, u32[]{:S(2)}) copy-start(f32[2,3,2,3,49]{4,2,3,1,0:T(2,128)} %param.14) | copy-start | bytes 21172
  16.4 1.9 %collective-permute-start.1 = (bf16[576,192]{1,0:T(8,128)(2,1)}, bf16[576,192]{1,0:T(8,128)(2,1)S(1)}, u32[]{:S(2)}, u32[]{:S(2)}) collective-permute-start(bf16[576,192]{1,0:T(8,128)(2,1)} %get-tuple-element.13.quads_hbm), channel_id=1, source_target_pairs={{0,1},{1,0},{2,3},{3,2},{4,5},{5,4},{6,7},{7,6},{8,9},{9,8},{10,11... | collective-permute-start | bytes 663560 | tf_op jit(solution)/shard_map/ppermute | solution.py:811
  16.9 1.6 %collective-permute-start = (bf16[16,48,128]{2,1,0:T(8,128)(2,1)S(1)}, bf16[16,48,128]{2,1,0:T(8,128)(2,1)S(1)}, u32[]{:S(2)}, u32[]{:S(2)}) collective-permute-start(bf16[16,48,128]{2,1,0:T(8,128)(2,1)S(1)} %all-to-all-done.own_ref), channel_id=1, source_target_pairs={{0,1},{1,0},{2,3},{3,2},{4,5},{5,4},{6,7},{7,6},{8,9},{9,8},{10,11... | collective-permute-start | bytes 589832 | tf_op jit(solution)/shard_map/ppermute | solution.py:813
  18.3 0.7 %copy-start.1 = (bf16[576,192]{1,0:T(8,128)(2,1)}, bf16[576,192]{1,0:T(8,128)(2,1)S(1)}, u32[]{:S(2)}) copy-start(bf16[576,192]{1,0:T(8,128)(2,1)S(1)} %collective-permute-done.1.other_quads_hbm) | copy-start | bytes 663556

commit v3 on v2

--- a/solution.py
+++ b/solution.py
@@ -203,6 +203,12 @@
     turns = np.arange(waves)[:, None] * np.arange(points)[None, :] % points
     angles = turns * (2.0 * np.pi / points)
     return np.concatenate([np.cos(angles), -np.sin(angles)]) * amplitude
+
+
+def folded(table, side):
+    near = table[: table.shape[0] // 2]
+    middle = table.shape[1] // 2
+    return 0.5 * near[:, :middle] + side * near[:, middle:]
 
 
 def matmul(a, b):
@@ -373,11 +379,11 @@
 
 
 def tables_kernel(z, layout, rate_ref, fold_smem, *refs):
-    inputs, outputs, scratch = refs[:10], refs[10:13], refs[13:]
+    inputs, outputs, scratch = refs[:9], refs[9:12], refs[12:]
     (scaled_s, sems), staged = scratch[:2], scratch[2:]
     copies = copies_in(inputs, staged, sems)
-    fold_ref, coef_ref, basis_ref, spread_ref, coarse_spread_ref = staged[:5]
-    sampled_ref, coarse_sampled_ref, from_ref, to_ref, picks_ref = staged[5:]
+    fold_ref, coef_ref, basis_ref, spread_ref = staged[:4]
+    sampled_ref, coarse_sampled_ref, from_ref, to_ref, picks_ref = staged[4:]
     out = named(z, *outputs)
     bf, f32 = jnp.bfloat16, jnp.float32
     lev = lax.axis_index("lev")
@@ -441,20 +447,35 @@
     coarse_hot = one_hot(z.coarse_columns, 1, coarse)
     short, long = 2 * coarse, 2 * (waves - coarse)
     levels = [(2 * x + core) * z.lev_dev + al for x in range(z.n_pair) for al in range(z.lev_dev)]
-    chunk = 2 * LANES
-    for begin in range(0, basis_ref.shape[1], chunk):
-        values = basis_ref[:, begin : begin + chunk].astype(f32)
-        for a, level in enumerate(levels):
-            scaled = coef_ref[pl.ds(level, 1), begin : begin + chunk] * values
-            scaled_s[a * short : (a + 1) * short, begin : begin + chunk] = scaled[:short].astype(bf)
-            at = z.own_levels * short + a * long
-            scaled_s[at : at + long, begin : begin + chunk] = scaled[short:].astype(bf)
+    period = basis_ref.shape[1]
+    row = lax.broadcasted_iota(jnp.int32, (2 * waves, 1), 0)
+    count = jnp.where(row < short, coarse, waves - coarse)
+    wave = jnp.where(row < short, row, row - short)
+    wave = jnp.where(wave < count, wave, wave - count) + jnp.where(row < short, 0, coarse)
+    sign = (1 - 2 * (wave & 1)).astype(f32)
+    chunk = LANES
+    lines = [coef_ref[pl.ds(level, 1), :] for level in levels]
+    for begin in range(0, period, chunk):
+        span = slice(begin, begin + chunk)
+        values = basis_ref[:, span].astype(f32)
+        signed = values * sign
+        for a, line in enumerate(lines):
+            near = line[:, span] * values
+            far = line[:, period + begin : period + begin + chunk] * signed
+            for side, scaled in enumerate((near + far, near - far)):
+                scaled_s[side, a * short : (a + 1) * short, span] = scaled[:short].astype(bf)
+                at = z.own_levels * short + a * long
+                scaled_s[side, at : at + long, span] = scaled[short:].astype(bf)
     for copy in copies[3:]:
         copy.wait()
     out["wave"].put(matmul_nt(sampled_ref[...], hot).astype(bf))
     out["coarse_wave"].put(matmul_nt(coarse_sampled_ref[...], coarse_hot).astype(bf))
-    coarse_quad = matmul(scaled_s[: z.own_levels * short, :], coarse_spread_ref[...]).astype(bf)
-    quad = matmul(scaled_s[...], spread_ref[...]).astype(bf)
+    even = matmul(scaled_s[0], spread_ref[0])
+    odd = matmul(scaled_s[1], spread_ref[1])
+    total, delta = even + odd, even - odd
+    middle, top = z.points // 2, z.own_levels * short
+    quad = jnp.concatenate([total[:, :middle], delta[:, :middle]], 1).astype(bf)
+    coarse_quad = jnp.concatenate([total[:top, middle:], delta[:top, middle:]], 1).astype(bf)
     for a in range(z.own_levels):
         at = z.own_levels * short + a * long
         pair = jnp.concatenate([quad[a * short : (a + 1) * short], quad[at : at + long]], 0)
@@ -464,8 +485,8 @@
         out["coarse_quad"].put(values, a * values.shape[0])
 
     def pick(name, index=0):
-        at, rows, columns = layout[name]
-        return picks_ref[pl.ds(pl.multiple_of(at + index * rows, SUBLANES), rows), :columns]
+        at, height, count, columns = layout[name]
+        return picks_ref[pl.ds(pl.multiple_of(at + index * height, 2 * SUBLANES), count), :columns]
 
     def mix(left, matrix, right, mask):
         return mix_matrix(left, matrix[...], right, mask)
@@ -557,11 +578,16 @@
     picked = ((lane == z.used) | (lane == z.used + 1)).astype(bf)
     gauss = matmul_nt(picked, legendre_s[0])[:1]
 
+    inner = 2 * sum(z.head + (s + 1) * z.rest <= LANES for s in range(slots))
+    spans = [(0, inner, LANES), (inner, 2 * slots, wide)]
     copies[0].wait()
     for w in range(z.n_wave):
         state = state_s[w]
-        left = jnp.concatenate([state * member(w, j) for j in range(2 * slots)], 0).astype(bf)
-        fourier_s[w * 2 * slots * rows : (w + 1) * 2 * slots * rows, :] = matmul_nt(left, legendre_s[w])
+        for first, last, width in spans:
+            left = [state[:, :width] * member(w, j)[:, :width] for j in range(first, last)]
+            left = jnp.concatenate(left, 0).astype(bf)
+            at = (w * 2 * slots + first) * rows
+            fourier_s[at : at + left.shape[0], :] = matmul_nt(left, legendre_s[w, :, :width])
 
     for copy in copies[1:]:
         copy.wait()
@@ -583,20 +609,24 @@
 
     stacked = []
     for w in range(z.n_wave):
-        left = jnp.concatenate(
-            [
+        outs = []
+        for first, last, width in spans:
+            left = [
                 back_s[pl.ds(w * 2 * slots + j, rows, stride=z.fine_columns), :].astype(bf)
-                for j in range(2 * slots)
-            ],
-            0,
-        )
-        out = matmul(left, legendre_s[w])
-        total = out[:rows]
-        for j in range(1, 2 * slots):
-            total = jnp.where(member(w, j) > 0.5, out[j * rows : (j + 1) * rows], total)
-        tend_s[w, :rows, :] = total
+                for j in range(first, last)
+            ]
+            out = matmul(jnp.concatenate(left, 0), legendre_s[w, :, :width])
+            outs += [out[i * rows : (i + 1) * rows] for i in range(last - first)]
+        total, beyond = outs[-1][:, :LANES], outs[-1][:, LANES:]
+        for j in range(2 * slots - 1):
+            chosen = member(w, j) > 0.5
+            total = jnp.where(chosen[:, :LANES], outs[j][:, :LANES], total)
+            if j >= inner:
+                beyond = jnp.where(chosen[:, LANES:], outs[j][:, LANES:], beyond)
+        tend_s[w, :rows, :LANES] = total
+        tend_s[w, :rows, LANES:] = beyond
         stacked.append(state_s[w][:, :LANES] * keep(w))
-        stacked.append(total[:, :LANES] * keep(w))
+        stacked.append(total * keep(w))
 
     modes = matmul_split(table["mix_to"].get(), jnp.concatenate(stacked, 1))
     evals, later, old_of, mid_of = [], [], [], []
@@ -641,37 +671,31 @@
             ]
             pieces.append(jnp.concatenate(piece, 0).astype(bf))
         grid = matmul(table["coarse_wave"].get(), jnp.concatenate(pieces, 1))
-        coarse_product_s[a] = (grid * grid).astype(bf)
+        before, fresh = grid[:, :LANES], grid[:, LANES:]
+        coarse_product_s[a] = (fresh * fresh - before * before).astype(bf)
     for a in range(z.levels):
         back = matmul(quad("coarse_quad", a, both_c), coarse_product_s[a])
-        for e in range(2):
-            values = back[:, e * LANES : (e + 1) * LANES] * gauss
-            coarse_back_s[e, a * both_c : (a + 1) * both_c, :] = values
+        coarse_back_s[a * both_c : (a + 1) * both_c, :] = back * gauss
 
     tends = []
     for w in range(z.n_wave):
         left = jnp.concatenate(
             [
-                coarse_back_s[e, pl.ds(w * slots + s, per_node, stride=z.coarse_columns), :].astype(bf)
+                coarse_back_s[pl.ds(w * slots + s, per_node, stride=z.coarse_columns), :].astype(bf)
                 for s in range(slots)
-                for e in range(2)
             ],
             0,
         )
         out = matmul(left, legendre_s[w, :, :LANES])
-        for e in range(2):
-            total = None
-            for s in range(slots):
-                at = (s * 2 + e) * per_node
-                term = slot(w, s) * out[at : at + per_node]
-                total = term if total is None else total + term
-            tends.append(total)
+        total = None
+        for s in range(slots):
+            term = slot(w, s) * out[s * per_node : (s + 1) * per_node]
+            total = term if total is None else total + term
+        tends.append(total)
     coarse_modes = matmul_split(table["mix_back"].get(), jnp.concatenate(tends, 1))
     for w in range(z.n_wave):
-        before = coarse_modes[:, 2 * w * LANES : (2 * w + 1) * LANES]
-        fresh = coarse_modes[:, (2 * w + 1) * LANES : (2 * w + 2) * LANES]
         end, inverse = later[w]
-        end = (end + STEP_HALF * (fresh - before)) * inverse
+        end = (end + STEP_HALF * coarse_modes[:, w * LANES : (w + 1) * LANES]) * inverse
         change_s[w, :per_node, :] = mid_of[w] - old_of[w][1]
         change_s[w, per_node:, :] = end - old_of[w][2]
 
@@ -741,11 +765,11 @@
     layout, rows, at = {}, [], 0
     for name, members in constants.items():
         count, columns = members[0].shape
-        height = round_up(count, SUBLANES)
-        layout[name] = (at, height, columns)
+        height = round_up(count, 2 * SUBLANES)
+        layout[name] = (at, height, count, columns)
         at += height * len(members)
         rows += [np.pad(m, ((0, height - count), (0, wide - columns))) for m in members]
-    return layout, jnp.asarray(np.concatenate(rows), jnp.float32)
+    return layout, jnp.asarray(np.concatenate(rows), jnp.bfloat16)
 
 
 def replicated_plan(
@@ -786,9 +810,16 @@
     coarse_spread = interpolation(z.coarse_points, longitudes, 2 * (z.coarse - 1))
     coarse_spread *= 2.0 * z.coarse / (longitudes // 2) * (coarse_amp / fine_amp)
     coarse_spread[1::2] = 0.0
+    spread = np.stack(
+        [
+            np.concatenate([folded(spread, side), folded(coarse_spread, side)], 1)
+            for side in (0.5, -0.5)
+        ]
+    )
     sampled = wave_rows(z.fine_width, z.points, fine_amp)[order].T
     coarse_sampled = wave_rows(z.coarse, z.coarse_points, coarse_amp).T
-    constants = [jnp.asarray(c, bf) for c in (basis, spread, coarse_spread, sampled, coarse_sampled)]
+    basis = basis[:, : longitudes // 2]
+    constants = [jnp.asarray(c, bf) for c in (basis, spread, sampled, coarse_sampled)]
     layout, picks = mix_constants(z)
     staged = [fold_pairs[None], grid_coef, *constants, modes_from, modes_to, picks]
     wide = 2 * LANES
@@ -799,7 +830,7 @@
         in_specs=[smem, smem] + [hbm] * len(staged),
         out_specs=(vmem,) * 3,
         scratch_shapes=[
-            pltpu.VMEM((z.own_levels * 2 * z.fine_width, longitudes), bf),
+            pltpu.VMEM((2, z.own_levels * 2 * z.fine_width, longitudes // 2), bf),
             pltpu.SemaphoreType.DMA((len(staged),)),
         ]
         + [pltpu.VMEM(array.shape, array.dtype) for array in staged],
@@ -828,7 +859,7 @@
             pltpu.VMEM((z.rows * z.fine_columns, lat_rows), f32),
             pltpu.VMEM((z.n_wave, z.rows + SUBLANES, wide), f32),
             pltpu.VMEM((2 * z.per_node * z.coarse_columns, lat_rows), f32),
-            pltpu.VMEM((2, z.per_node * z.coarse_columns, lat_rows), f32),
+            pltpu.VMEM((z.per_node * z.coarse_columns, lat_rows), f32),
             pltpu.VMEM((z.n_wave, (z.nodes - 1) * z.per_node, LANES), f32),
             pltpu.VMEM(narrow_shape, bf),
             pltpu.VMEM(full_shape, f32),
@@ -837,7 +868,7 @@
             pltpu.SemaphoreType.DMA((4,)),
             pltpu.VMEM((z.n_wave, lat_rows, wide), bf),
             pltpu.VMEM((z.levels, z.points, z.nodes * LANES), bf),
-            pltpu.VMEM((z.levels, z.coarse_points, 2 * LANES), bf),
+            pltpu.VMEM((z.levels, z.coarse_points, LANES), bf),
         ],
         compiler_params=pltpu.CompilerParams(vmem_limit_bytes=VMEM_BYTES),
         name="sweep",
@@ -856,6 +887,7 @@
         and z.used > LANES
         and z.used + 2 - LANES <= z.unit
         and z.lats % SUBLANES == 0
+        and z.head + z.rest <= LANES
         and n_lev * z.lats <= LANES
         and gathered <= REPLICATED_BYTES
     )

time: 24.4 us -> 23.7 us (0.971)
  Pallas kernels: 12 us -> 11.3 us
  waiting for transfers between devices: 2.01 us -> 2.53 us
  local copies, waits for them, and re-layouts: 0.44 us -> 0.01 us
    pallas_call x1, Pallas kernels: 5.31 us -> 4.67 us  [replicated_plan(): pl.pallas_call(functools.partial(tables_kernel, z, layout), out_shape=(sh...]
    all_to_all x1, waiting for transfers between devices: 0.46 us -> 1.09 us  [replicated_plan(): lax.all_to_all(block, ('wave', 'lev'), 0, 0, tiled=True, axis_index_group...]
    ppermute x1, waiting for transfers between devices: 1.28 us -> 0.69 us  [replicated_plan(): other_quads = lax.ppermute(quads, ('wave', 'lev'), partners)]
    ppermute x1, waiting for transfers between devices: 0.28 us -> 0.75 us  [replicated_plan(): other = lax.ppermute(own, ('wave', 'lev'), partners)]
    unnamed x4, local copies, waits for them, and re-layouts: 0.44 us -> 0.01 us
  transfers between devices with their start and end apart: 3 -> 3, of which waited for: 3 -> 3; matrix products, arithmetic and copies ran while one was open for 0% -> 0% of each run, Pallas kernels for 22% -> 20%
where the time goes in v3:
time: 23.7 us; the launch traced here: 23.4 us
  Pallas kernels  11.3 us (48%)
  starting transfers between devices  8.9 us (38%)
  waiting for transfers between devices  2.53 us (11%)
  between operations  0.66 us (3%)
    all_to_all x1, starting transfers between devices, replicated_plan(): lax.all_to_all(block, ('wave', 'lev'), 0, 0, tiled=True, axis_index_group...  8.82 us
    pallas_call x1, Pallas kernels, replicated_plan(): pl.pallas_call(functools.partial(sweep_kernel, z), out_shape=(shape((z.le...  4.97 us
    pallas_call x1, Pallas kernels, replicated_plan(): pl.pallas_call(functools.partial(tables_kernel, z, layout), out_shape=(sh...  4.67 us
    pallas_call x1, Pallas kernels, replicated_plan(): pl.pallas_call(functools.partial(pack_kernel, z), out_shape=shape((z.chip...  1.63 us
    all_to_all x1, waiting for transfers between devices, replicated_plan(): lax.all_to_all(block, ('wave', 'lev'), 0, 0, tiled=True, axis_index_group...  1.09 us
    ppermute x1, waiting for transfers between devices, replicated_plan(): other = lax.ppermute(own, ('wave', 'lev'), partners)  0.75 us
    ppermute x1, waiting for transfers between devices, replicated_plan(): other_quads = lax.ppermute(quads, ('wave', 'lev'), partners)  0.69 us
  transfers between devices with their start and end apart: 3, of which 3 were waited for; matrix products, arithmetic and copies ran while one was open for 0% of the time, Pallas kernels for 20%

profile of v3, /device:TPU:0, one launch (start us, length us, event | category | flops | bytes accessed | tf_op | source)
XLA Modules:
  0.0 23.4 jit_solution(15530622205704944819)
XLA Ops:
  0.6 1.6 %pack.1 = bf16[16,48,128]{2,1,0:T(8,128)(2,1)} custom-call(f32[2,3,3,2,49]{4,3,2,1,0:T(2,128)} %bitcast.5, bf16[3,24,49]{2,1,0:T(8,128)(2,1)} %leg_hbm.1, f32[1,24]{1,0:T(1,128)} %bitcast.7), custom_call_target="tpu_custom_call" | custom-call | tf_op jit(solution)/shard_map/pack/pallas_call | solution.py:786
  2.3 8.8 %all-to-all-start = ((bf16[16,48,128]{2,1,0:T(8,128)(2,1)}), bf16[16,48,128]{2,1,0:T(8,128)(2,1)S(1)}, u32[]{:S(2)}, u32[]{:S(2)}) async-start(bf16[16,48,128]{2,1,0:T(8,128)(2,1)} %pack.1), calls=%async_computation | async-start | bytes 393216 | tf_op jit(solution)/shard_map/all_to_all | solution.py:801
  11.1 0.0 copy-start
  11.1 4.7 %tables.1 = (bf16[384,144]{1,0:T(8,128)(2,1)}, f32[352,256]{1,0:T(8,128)}, bf16[576,192]{1,0:T(8,128)(2,1)}) custom-call(f32[8]{0:T(128)} %rate_ref.1, s32[24]{0:T(128)} %fold_smem.1, s32[1,24]{1,0:T(1,128)} %bitcast.10, f32[8,2560]{1,0:T(8,128)} %refs_1_.1, bf16[96,1280]{1,0:T(8,128)(2,1)} %constant.10.clone.refs_2_, ...), custom_call_target="tpu_custom_call" | custom-call | flops 1000000000 | bytes 4000000 | tf_op jit(solution)/shard_map/tables/pallas_call | solution.py:827
  15.8 0.1 collective-permute-start.1
  15.9 1.1 %all-to-all-done.own_ref = bf16[16,48,128]{2,1,0:T(8,128)(2,1)S(1)} async-done(((bf16[16,48,128]{2,1,0:T(8,128)(2,1)}), bf16[16,48,128]{2,1,0:T(8,128)(2,1)S(1)}, u32[]{:S(2)}, u32[]{:S(2)}) %all-to-all-start) | async-done | bytes 196640 | tf_op jit(solution)/shard_map/all_to_all | solution.py:801
  16.9 0.0 collective-permute-start
  16.9 0.7 %collective-permute-done.1.other_quads_hbm = bf16[576,192]{1,0:T(8,128)(2,1)S(1)} collective-permute-done((bf16[576,192]{1,0:T(8,128)(2,1)}, bf16[576,192]{1,0:T(8,128)(2,1)S(1)}, u32[]{:S(2)}, u32[]{:S(2)}) %collective-permute-start.1) | collective-permute-done | bytes 221216 | tf_op jit(solution)/shard_map/ppermute | solution.py:842
  17.6 0.0 copy-start.1
  17.6 0.8 %collective-permute-done.other_ref = bf16[16,48,128]{2,1,0:T(8,128)(2,1)S(1)} collective-permute-done((bf16[16,48,128]{2,1,0:T(8,128)(2,1)S(1)}, bf16[16,48,128]{2,1,0:T(8,128)(2,1)S(1)}, u32[]{:S(2)}, u32[]{:S(2)}) %collective-permute-start) | collective-permute-done | bytes 196640 | tf_op jit(solution)/shard_map/ppermute | solution.py:844
  18.4 0.0 copy-done.1
  18.4 0.0 copy-done
  18.4 5.0 %sweep.1 = (f32[2,2,3,2,49]{4,3,2,1,0:T(2,128)}, f32[2,3,3,2,49]{4,3,2,1,0:T(2,128)}) custom-call(bf16[16,48,128]{2,1,0:T(8,128)(2,1)S(1)} %all-to-all-done.own_ref, bf16[16,48,128]{2,1,0:T(8,128)(2,1)S(1)} %collective-permute-done.other_ref, f32[2,3,3,2,49]{4,3,2,1,0:T(2,128)S(1)} %bitcast.6, bf16[384,144]{1,0:T(8,128)(2,1)} %get-tuple-element.11.narrow_hbm, ...), custom_call_target="tpu_custom_call" | custom-call | tf_op jit(solution)/shard_map/sweep/pallas_call | solution.py:847
Async XLA Ops:
  2.3 14.7 %all-to-all-start = ((bf16[16,48,128]{2,1,0:T(8,128)(2,1)}), bf16[16,48,128]{2,1,0:T(8,128)(2,1)S(1)}, u32[]{:S(2)}, u32[]{:S(2)}) async-start(bf16[16,48,128]{2,1,0:T(8,128)(2,1)} %pack.1), calls=%async_computation | async-start | bytes 393216 | tf_op jit(solution)/shard_map/all_to_all | solution.py:801
  11.1 7.3 %copy-start = (f32[2,3,2,3,49]{4,2,3,1,0:T(2,128)S(1)}, f32[2,3,2,3,49]{4,2,3,1,0:T(2,128)}, u32[]{:S(2)}) copy-start(f32[2,3,2,3,49]{4,2,3,1,0:T(2,128)} %param.13) | copy-start | bytes 21172
  15.8 1.9 %collective-permute-start.1 = (bf16[576,192]{1,0:T(8,128)(2,1)}, bf16[576,192]{1,0:T(8,128)(2,1)S(1)}, u32[]{:S(2)}, u32[]{:S(2)}) collective-permute-start(bf16[576,192]{1,0:T(8,128)(2,1)} %get-tuple-element.13.quads_hbm), channel_id=1, source_target_pairs={{0,1},{1,0},{2,3},{3,2},{4,5},{5,4},{6,7},{7,6},{8,9},{9,8},{10,11... | collective-permute-start | bytes 663560 | tf_op jit(solution)/shard_map/ppermute | solution.py:842
  16.9 1.4 %collective-permute-start = (bf16[16,48,128]{2,1,0:T(8,128)(2,1)S(1)}, bf16[16,48,128]{2,1,0:T(8,128)(2,1)S(1)}, u32[]{:S(2)}, u32[]{:S(2)}) collective-permute-start(bf16[16,48,128]{2,1,0:T(8,128)(2,1)S(1)} %all-to-all-done.own_ref), channel_id=1, source_target_pairs={{0,1},{1,0},{2,3},{3,2},{4,5},{5,4},{6,7},{7,6},{8,9},{9,8},{10,11... | collective-permute-start | bytes 589832 | tf_op jit(solution)/shard_map/ppermute | solution.py:844
  17.6 0.8 %copy-start.1 = (bf16[576,192]{1,0:T(8,128)(2,1)}, bf16[576,192]{1,0:T(8,128)(2,1)S(1)}, u32[]{:S(2)}) copy-start(bf16[576,192]{1,0:T(8,128)(2,1)S(1)} %collective-permute-done.1.other_quads_hbm) | copy-start | bytes 663556

commit v4 on v3

--- a/solution.py
+++ b/solution.py
@@ -231,6 +231,10 @@
 def matmul_split(left, right):
     high, low = high_low(right)
     return matmul(left, jnp.concatenate([high, low, high], 0))
+
+
+def pitch(count):
+    return count + 4 if count % 8 == 0 else count
 
 
 class Sizes:
@@ -259,6 +263,10 @@
         self.position = [self.order.index(i) for i in range(self.chips)]
         self.fine_columns = self.n_wave * self.slots * 2
         self.coarse_columns = self.n_wave * self.slots
+        self.row_pitch = pitch(self.rows)
+        self.column_pitch = pitch(self.fine_columns)
+        self.mode_pitch = pitch(2 * self.per_node)
+        self.slot_pitch = pitch(self.coarse_columns)
         self.points = round_up(4 * (self.fine_width - 1) + 1, 32)
         self.coarse_points = round_up(4 * (self.coarse - 1) + 1, 32)
 
@@ -529,9 +537,11 @@
     slots, rows, lats, per_node = z.slots, z.rows, z.lats, z.per_node
     table = named(z, narrow_ref, full_ref)
     quads = [named(z, *[ref] * 3) for ref in (quads_ref, other_quads_ref)]
+    masks = pl.ds(0, z.fine_columns)
+    others = pl.ds(z.fine_columns, full_ref.shape[0] - z.fine_columns)
     copies = copies_in(
-        (full_hbm, narrow_hbm, quads_hbm, other_quads_hbm),
-        (full_ref, narrow_ref, quads_ref, other_quads_ref),
+        (full_hbm.at[masks], narrow_hbm, full_hbm.at[others], quads_hbm, other_quads_hbm),
+        (full_ref.at[masks], narrow_ref, full_ref.at[others], quads_ref, other_quads_ref),
         sems,
     )
 
@@ -586,8 +596,10 @@
         for first, last, width in spans:
             left = [state[:, :width] * member(w, j)[:, :width] for j in range(first, last)]
             left = jnp.concatenate(left, 0).astype(bf)
-            at = (w * 2 * slots + first) * rows
-            fourier_s[at : at + left.shape[0], :] = matmul_nt(left, legendre_s[w, :, :width])
+            out = matmul_nt(left, legendre_s[w, :, :width])
+            for j in range(first, last):
+                at = (w * 2 * slots + j) * z.row_pitch
+                fourier_s[at : at + rows, :] = out[(j - first) * rows : (j - first + 1) * rows]
 
     for copy in copies[1:]:
         copy.wait()
@@ -597,7 +609,7 @@
         pieces = []
         for b in range(z.nodes):
             at = (a * z.nodes + b) * 2
-            piece = [fourier_s[pl.ds(at + c, half, stride=rows), :] for c in range(2)]
+            piece = [fourier_s[pl.ds(at + c, half, stride=z.row_pitch), :] for c in range(2)]
             pieces.append(jnp.concatenate(piece, 0).astype(bf))
         grid = matmul(table["wave"].get(), jnp.concatenate(pieces, 1))
         product_s[a] = (grid * grid).astype(bf)
@@ -605,14 +617,16 @@
         back = matmul(quad("quad", a, both), product_s[a])
         for b in range(z.nodes):
             values = back[:, b * LANES : (b + 1) * LANES] * gauss
-            back_s[(a * z.nodes + b) * both : (a * z.nodes + b + 1) * both, :] = values
+            for c in range(2):
+                at = ((a * z.nodes + b) * 2 + c) * z.column_pitch
+                back_s[at : at + half, :] = values[c * half : (c + 1) * half]
 
     stacked = []
     for w in range(z.n_wave):
         outs = []
         for first, last, width in spans:
             left = [
-                back_s[pl.ds(w * 2 * slots + j, rows, stride=z.fine_columns), :].astype(bf)
+                back_s[pl.ds(w * 2 * slots + j, rows, stride=z.column_pitch), :].astype(bf)
                 for j in range(first, last)
             ]
             out = matmul(jnp.concatenate(left, 0), legendre_s[w, :, :width])
@@ -659,7 +673,9 @@
             0,
         ).astype(bf)
         out = matmul_nt(left, legendre_s[w, :, :LANES])
-        coarse_s[w * slots * 2 * per_node : (w + 1) * slots * 2 * per_node, :] = out
+        for s in range(slots):
+            at = (w * slots + s) * z.mode_pitch
+            coarse_s[at : at + 2 * per_node, :] = out[s * 2 * per_node : (s + 1) * 2 * per_node]
 
     both_c = 2 * z.coarse_columns
     for a in range(z.levels):
@@ -667,7 +683,7 @@
         for e in range(2):
             at = e * per_node + a * 2
             piece = [
-                coarse_s[pl.ds(at + c, z.coarse_columns, stride=2 * per_node), :] for c in range(2)
+                coarse_s[pl.ds(at + c, z.coarse_columns, stride=z.mode_pitch), :] for c in range(2)
             ]
             pieces.append(jnp.concatenate(piece, 0).astype(bf))
         grid = matmul(table["coarse_wave"].get(), jnp.concatenate(pieces, 1))
@@ -675,13 +691,16 @@
         coarse_product_s[a] = (fresh * fresh - before * before).astype(bf)
     for a in range(z.levels):
         back = matmul(quad("coarse_quad", a, both_c), coarse_product_s[a])
-        coarse_back_s[a * both_c : (a + 1) * both_c, :] = back * gauss
+        values = back * gauss
+        for c in range(2):
+            at = (a * 2 + c) * z.slot_pitch
+            coarse_back_s[at : at + z.coarse_columns, :] = values[c * z.coarse_columns :][: z.coarse_columns]
 
     tends = []
     for w in range(z.n_wave):
         left = jnp.concatenate(
             [
-                coarse_back_s[pl.ds(w * slots + s, per_node, stride=z.coarse_columns), :].astype(bf)
+                coarse_back_s[pl.ds(w * slots + s, per_node, stride=z.slot_pitch), :].astype(bf)
                 for s in range(slots)
             ],
             0,
@@ -855,17 +874,17 @@
         scratch_shapes=[
             pltpu.VMEM((z.n_wave, lat_rows, wide), f32),
             pltpu.VMEM((z.n_wave, z.rows, wide), f32),
-            pltpu.VMEM((z.rows * z.fine_columns, lat_rows), f32),
-            pltpu.VMEM((z.rows * z.fine_columns, lat_rows), f32),
+            pltpu.VMEM((z.row_pitch * z.fine_columns, lat_rows), f32),
+            pltpu.VMEM((z.rows * z.column_pitch, lat_rows), f32),
             pltpu.VMEM((z.n_wave, z.rows + SUBLANES, wide), f32),
-            pltpu.VMEM((2 * z.per_node * z.coarse_columns, lat_rows), f32),
-            pltpu.VMEM((z.per_node * z.coarse_columns, lat_rows), f32),
+            pltpu.VMEM((z.mode_pitch * z.coarse_columns, lat_rows), f32),
+            pltpu.VMEM((z.per_node * z.slot_pitch, lat_rows), f32),
             pltpu.VMEM((z.n_wave, (z.nodes - 1) * z.per_node, LANES), f32),
             pltpu.VMEM(narrow_shape, bf),
             pltpu.VMEM(full_shape, f32),
             pltpu.VMEM(quads_shape, bf),
             pltpu.VMEM(quads_shape, bf),
-            pltpu.SemaphoreType.DMA((4,)),
+            pltpu.SemaphoreType.DMA((5,)),
             pltpu.VMEM((z.n_wave, lat_rows, wide), bf),
             pltpu.VMEM((z.levels, z.points, z.nodes * LANES), bf),
             pltpu.VMEM((z.levels, z.coarse_points, LANES), bf),

time: 23.7 us -> 23.2 us (0.979)
  Pallas kernels: 11.3 us -> 10.7 us
    pallas_call x1, Pallas kernels: 4.97 us -> 4.44 us  [replicated_plan(): pl.pallas_call(functools.partial(sweep_kernel, z), out_shape=(shape((z.le...]
where the time goes in v4:
time: 23.2 us; the launch traced here: 22.8 us
  Pallas kernels  10.7 us (46%)
  starting transfers between devices  8.9 us (38%)
  waiting for transfers between devices  2.53 us (11%)
  between operations  0.66 us (3%)
    all_to_all x1, starting transfers between devices, replicated_plan(): lax.all_to_all(block, ('wave', 'lev'), 0, 0, tiled=True, axis_index_group...  8.82 us
    pallas_call x1, Pallas kernels, replicated_plan(): pl.pallas_call(functools.partial(tables_kernel, z, layout), out_shape=(sh...  4.67 us
    pallas_call x1, Pallas kernels, replicated_plan(): pl.pallas_call(functools.partial(sweep_kernel, z), out_shape=(shape((z.le...  4.44 us
    pallas_call x1, Pallas kernels, replicated_plan(): pl.pallas_call(functools.partial(pack_kernel, z), out_shape=shape((z.chip...  1.63 us
    all_to_all x1, waiting for transfers between devices, replicated_plan(): lax.all_to_all(block, ('wave', 'lev'), 0, 0, tiled=True, axis_index_group...  1.09 us
    ppermute x1, waiting for transfers between devices, replicated_plan(): other = lax.ppermute(own, ('wave', 'lev'), partners)  0.75 us
    ppermute x1, waiting for transfers between devices, replicated_plan(): other_quads = lax.ppermute(quads, ('wave', 'lev'), partners)  0.69 us
  transfers between devices with their start and end apart: 3, of which 3 were waited for; matrix products, arithmetic and copies ran while one was open for 0% of the time, Pallas kernels for 20%

profile of v4, /device:TPU:0, one launch (start us, length us, event | category | flops | bytes accessed | tf_op | source)
XLA Modules:
  0.0 22.8 jit_solution(12501368816714544580)
XLA Ops:
  0.6 1.6 %pack.1 = bf16[16,48,128]{2,1,0:T(8,128)(2,1)} custom-call(f32[2,3,3,2,49]{4,3,2,1,0:T(2,128)} %bitcast.5, bf16[3,24,49]{2,1,0:T(8,128)(2,1)} %leg_hbm.1, f32[1,24]{1,0:T(1,128)} %bitcast.7), custom_call_target="tpu_custom_call" | custom-call | tf_op jit(solution)/shard_map/pack/pallas_call | solution.py:805
  2.3 8.8 %all-to-all-start = ((bf16[16,48,128]{2,1,0:T(8,128)(2,1)}), bf16[16,48,128]{2,1,0:T(8,128)(2,1)S(1)}, u32[]{:S(2)}, u32[]{:S(2)}) async-start(bf16[16,48,128]{2,1,0:T(8,128)(2,1)} %pack.1), calls=%async_computation | async-start | bytes 393216 | tf_op jit(solution)/shard_map/all_to_all | solution.py:820
  11.1 0.0 copy-start
  11.1 4.7 %tables.1 = (bf16[384,144]{1,0:T(8,128)(2,1)}, f32[352,256]{1,0:T(8,128)}, bf16[576,192]{1,0:T(8,128)(2,1)}) custom-call(f32[8]{0:T(128)} %rate_ref.1, s32[24]{0:T(128)} %fold_smem.1, s32[1,24]{1,0:T(1,128)} %bitcast.10, f32[8,2560]{1,0:T(8,128)} %refs_1_.1, bf16[96,1280]{1,0:T(8,128)(2,1)} %constant.10.clone.refs_2_, ...), custom_call_target="tpu_custom_call" | custom-call | flops 1000000000 | bytes 4000000 | tf_op jit(solution)/shard_map/tables/pallas_call | solution.py:846
  15.8 0.1 collective-permute-start.1
  15.9 1.1 %all-to-all-done.own_ref = bf16[16,48,128]{2,1,0:T(8,128)(2,1)S(1)} async-done(((bf16[16,48,128]{2,1,0:T(8,128)(2,1)}), bf16[16,48,128]{2,1,0:T(8,128)(2,1)S(1)}, u32[]{:S(2)}, u32[]{:S(2)}) %all-to-all-start) | async-done | bytes 196640 | tf_op jit(solution)/shard_map/all_to_all | solution.py:820
  16.9 0.0 collective-permute-start
  16.9 0.7 %collective-permute-done.1.other_quads_hbm = bf16[576,192]{1,0:T(8,128)(2,1)S(1)} collective-permute-done((bf16[576,192]{1,0:T(8,128)(2,1)}, bf16[576,192]{1,0:T(8,128)(2,1)S(1)}, u32[]{:S(2)}, u32[]{:S(2)}) %collective-permute-start.1) | collective-permute-done | bytes 221216 | tf_op jit(solution)/shard_map/ppermute | solution.py:861
  17.6 0.0 copy-start.1
  17.6 0.8 %collective-permute-done.other_ref = bf16[16,48,128]{2,1,0:T(8,128)(2,1)S(1)} collective-permute-done((bf16[16,48,128]{2,1,0:T(8,128)(2,1)S(1)}, bf16[16,48,128]{2,1,0:T(8,128)(2,1)S(1)}, u32[]{:S(2)}, u32[]{:S(2)}) %collective-permute-start) | collective-permute-done | bytes 196640 | tf_op jit(solution)/shard_map/ppermute | solution.py:863
  18.4 0.0 copy-done.1
  18.4 0.0 copy-done
  18.4 4.4 %sweep.1 = (f32[2,2,3,2,49]{4,3,2,1,0:T(2,128)}, f32[2,3,3,2,49]{4,3,2,1,0:T(2,128)}) custom-call(bf16[16,48,128]{2,1,0:T(8,128)(2,1)S(1)} %all-to-all-done.own_ref, bf16[16,48,128]{2,1,0:T(8,128)(2,1)S(1)} %collective-permute-done.other_ref, f32[2,3,3,2,49]{4,3,2,1,0:T(2,128)S(1)} %bitcast.6, bf16[384,144]{1,0:T(8,128)(2,1)} %get-tuple-element.11.narrow_hbm, ...), custom_call_target="tpu_custom_call" | custom-call | tf_op jit(solution)/shard_map/sweep/pallas_call | solution.py:866
Async XLA Ops:
  2.3 14.7 %all-to-all-start = ((bf16[16,48,128]{2,1,0:T(8,128)(2,1)}), bf16[16,48,128]{2,1,0:T(8,128)(2,1)S(1)}, u32[]{:S(2)}, u32[]{:S(2)}) async-start(bf16[16,48,128]{2,1,0:T(8,128)(2,1)} %pack.1), calls=%async_computation | async-start | bytes 393216 | tf_op jit(solution)/shard_map/all_to_all | solution.py:820
  11.1 7.3 %copy-start = (f32[2,3,2,3,49]{4,2,3,1,0:T(2,128)S(1)}, f32[2,3,2,3,49]{4,2,3,1,0:T(2,128)}, u32[]{:S(2)}) copy-start(f32[2,3,2,3,49]{4,2,3,1,0:T(2,128)} %param.13) | copy-start | bytes 21172
  15.8 1.9 %collective-permute-start.1 = (bf16[576,192]{1,0:T(8,128)(2,1)}, bf16[576,192]{1,0:T(8,128)(2,1)S(1)}, u32[]{:S(2)}, u32[]{:S(2)}) collective-permute-start(bf16[576,192]{1,0:T(8,128)(2,1)} %get-tuple-element.13.quads_hbm), channel_id=1, source_target_pairs={{0,1},{1,0},{2,3},{3,2},{4,5},{5,4},{6,7},{7,6},{8,9},{9,8},{10,11... | collective-permute-start | bytes 663560 | tf_op jit(solution)/shard_map/ppermute | solution.py:861
  16.9 1.4 %collective-permute-start = (bf16[16,48,128]{2,1,0:T(8,128)(2,1)S(1)}, bf16[16,48,128]{2,1,0:T(8,128)(2,1)S(1)}, u32[]{:S(2)}, u32[]{:S(2)}) collective-permute-start(bf16[16,48,128]{2,1,0:T(8,128)(2,1)S(1)} %all-to-all-done.own_ref), channel_id=1, source_target_pairs={{0,1},{1,0},{2,3},{3,2},{4,5},{5,4},{6,7},{7,6},{8,9},{9,8},{10,11... | collective-permute-start | bytes 589832 | tf_op jit(solution)/shard_map/ppermute | solution.py:863
  17.6 0.8 %copy-start.1 = (bf16[576,192]{1,0:T(8,128)(2,1)}, bf16[576,192]{1,0:T(8,128)(2,1)S(1)}, u32[]{:S(2)}) copy-start(bf16[576,192]{1,0:T(8,128)(2,1)S(1)} %collective-permute-done.1.other_quads_hbm) | copy-start | bytes 663556

commit v5 on v4

--- a/solution.py
+++ b/solution.py
@@ -266,7 +266,7 @@
         self.row_pitch = pitch(self.rows)
         self.column_pitch = pitch(self.fine_columns)
         self.mode_pitch = pitch(2 * self.per_node)
-        self.slot_pitch = pitch(self.coarse_columns)
+        self.slot_pitch = round_up(self.per_node, SUBLANES) + SUBLANES
         self.points = round_up(4 * (self.fine_width - 1) + 1, 32)
         self.coarse_points = round_up(4 * (self.coarse - 1) + 1, 32)
 
@@ -284,8 +284,7 @@
         member=(z.fine_columns, 2 * LANES),
         slot=(z.coarse_columns, LANES),
         keep=(z.n_wave, LANES),
-        stiff=(z.n_wave * z.per_node, LANES),
-        inverse=(z.n_wave * z.per_node, LANES),
+        stiff=(z.n_wave * z.per_node, 2 * LANES),
     )
 
     def placed(shapes, unit):
@@ -309,6 +308,10 @@
     def get(self, begin=0, count=None):
         begin = self.at + begin
         return self.ref[begin : begin + (count or self.count), : self.columns]
+
+    def rows(self, block, count):
+        begin = pl.multiple_of(self.at + block * count, SUBLANES)
+        return self.ref[pl.ds(begin, count), : self.columns]
 
     def put(self, values, begin=0):
         begin = self.at + begin
@@ -386,12 +389,12 @@
     return (matmul(halves, pick_right.astype(bf)) * mask.astype(f32)).astype(bf)
 
 
-def tables_kernel(z, layout, rate_ref, fold_smem, *refs):
-    inputs, outputs, scratch = refs[:9], refs[9:12], refs[12:]
+def tables_kernel(z, layout, *refs):
+    inputs, outputs, scratch = refs[:10], refs[10:13], refs[13:]
     (scaled_s, sems), staged = scratch[:2], scratch[2:]
     copies = copies_in(inputs, staged, sems)
-    fold_ref, coef_ref, basis_ref, spread_ref = staged[:4]
-    sampled_ref, coarse_sampled_ref, from_ref, to_ref, picks_ref = staged[4:]
+    fold_ref, rate_ref, coef_ref, basis_ref, spread_ref = staged[:5]
+    sampled_ref, coarse_sampled_ref, from_ref, to_ref, picks_ref = staged[5:]
     out = named(z, *outputs)
     bf, f32 = jnp.bfloat16, jnp.float32
     lev = lax.axis_index("lev")
@@ -408,29 +411,36 @@
             inside = (lane >= begin) & (lane < begin + width)
             lane_slot = jnp.where(inside, s, lane_slot)
             lane_row = jnp.where(inside, lane - begin + first, lane_row)
-    rate_row = lax.broadcasted_iota(jnp.int32, (z.per_node, LANES), 0)
-    rates = jnp.zeros((z.per_node, LANES), f32)
-    for q in range(z.levels):
-        rates = jnp.where((rate_row >= 2 * q) & (rate_row < 2 * q + 2), rate_ref[q], rates)
+    copies[0].wait()
+    copies[1].wait()
+    wave_row = lax.broadcasted_iota(jnp.int32, (z.n_wave, z.coarse_columns), 0)
+    fold_lane = lax.broadcasted_iota(jnp.int32, (z.n_wave, z.coarse_columns), 1)
+    small = jnp.zeros((z.n_wave, wide), f32)
+    for s in range(z.slots):
+        chosen = jnp.where(fold_lane == wave_row * z.slots + s, fold_ref[...].astype(f32), 0.0)
+        small = jnp.where(lane_slot == s, jnp.sum(chosen, axis=1, keepdims=True), small)
+    lane_row = lane_row.astype(f32)
+    first = lane_row < waves - small
+    keep = (lane < z.head) & (lane_row < coarse - small)
+    out["keep"].put(keep[:, :LANES].astype(f32))
+    for s in range(z.slots):
+        own = lane_slot == s
+        at = 2 * s * z.n_wave
+        out["member"].put((own & first).astype(f32), at)
+        out["member"].put((own & jnp.logical_not(first)).astype(f32), at + z.n_wave)
+        out["slot"].put((own & keep)[:, :LANES].astype(f32), s * z.n_wave)
+    mode_row = lax.broadcasted_iota(jnp.int32, (z.per_node, z.levels), 0)
+    rate_lane = lax.broadcasted_iota(jnp.int32, (z.per_node, z.levels), 1)
+    chosen = jnp.where((mode_row >= 2 * rate_lane) & (mode_row < 2 * rate_lane + 2), rate_ref[...], 0.0)
+    rates = jnp.sum(chosen, axis=1, keepdims=True)
+    degree = (small + lane_row)[:, :LANES]
+    degree = degree * (degree + 1.0) / (coarse * (coarse + 1.0))
     for w in range(z.n_wave):
-        small = jnp.zeros((1, wide), jnp.int32)
-        for s in range(z.slots):
-            small = jnp.where(lane_slot == s, fold_smem[w * z.slots + s], small)
-        first = lane_row < waves - small
-        keep = (lane < z.head) & (lane_row < coarse - small)
-        out["keep"].put(keep[:, :LANES].astype(f32), w)
-        for s in range(z.slots):
-            own = lane_slot == s
-            at = (w * z.slots + s) * 2
-            out["member"].put((own & first).astype(f32), at)
-            out["member"].put((own & jnp.logical_not(first)).astype(f32), at + 1)
-            out["slot"].put((own & keep)[:, :LANES].astype(f32), w * z.slots + s)
-        degree = (small + lane_row)[:, :LANES].astype(f32)
-        stiff = rates * (degree * (degree + 1.0) / (coarse * (coarse + 1.0)))
-        out["stiff"].put(stiff, w * z.per_node)
-        out["inverse"].put(1.0 / (1.0 + STEP_HALF * stiff), w * z.per_node)
-
-    for copy in copies[:3]:
+        stiff = rates * degree[w : w + 1]
+        both = jnp.concatenate([stiff, 1.0 / (1.0 + STEP_HALF * stiff)], 1)
+        out["stiff"].put(both, w * z.per_node)
+
+    for copy in copies[2:4]:
         copy.wait()
 
     def wave_column(count, per_slot):
@@ -474,7 +484,7 @@
                 scaled_s[side, a * short : (a + 1) * short, span] = scaled[:short].astype(bf)
                 at = z.own_levels * short + a * long
                 scaled_s[side, at : at + long, span] = scaled[short:].astype(bf)
-    for copy in copies[3:]:
+    for copy in copies[4:]:
         copy.wait()
     out["wave"].put(matmul_nt(sampled_ref[...], hot).astype(bf))
     out["coarse_wave"].put(matmul_nt(coarse_sampled_ref[...], coarse_hot).astype(bf))
@@ -523,7 +533,7 @@
     tend_s,
     coarse_s,
     coarse_back_s,
-    change_s,
+    modes_s,
     narrow_ref,
     full_ref,
     quads_ref,
@@ -553,10 +563,10 @@
     all_lats = z.n_lev * lats
 
     def member(w, j):
-        return table["member"].get(w * slots * 2 + j, 1)
+        return table["member"].get(j * z.n_wave + w, 1)
 
     def slot(w, s):
-        return table["slot"].get(w * slots + s, 1)
+        return table["slot"].get(s * z.n_wave + w, 1)
 
     def keep(w):
         return table["keep"].get(w, 1)
@@ -643,24 +653,26 @@
         stacked.append(total * keep(w))
 
     modes = matmul_split(table["mix_to"].get(), jnp.concatenate(stacked, 1))
-    evals, later, old_of, mid_of = [], [], [], []
     for w in range(z.n_wave):
+        modes_s[w] = modes[:, 2 * w * LANES : 2 * (w + 1) * LANES]
+
+    def advance(part, both_stiff):
+        stiff, inverse = both_stiff[:, :LANES], both_stiff[:, LANES:]
         old, source = [], []
-        stiff = table["stiff"].get(w * per_node, per_node)
         for b in range(z.nodes):
-            part = modes[b * per_node : (b + 1) * per_node]
-            old.append(part[:, 2 * w * LANES : (2 * w + 1) * LANES])
-            source.append(part[:, (2 * w + 1) * LANES : (2 * w + 2) * LANES] - stiff * old[-1])
-        inverse = table["inverse"].get(w * per_node, per_node)
+            values = part[b * per_node : (b + 1) * per_node]
+            old.append(values[:, :LANES])
+            source.append(values[:, LANES:] - stiff * old[-1])
         mid = sum(quad_weights[0][b] * source[b] for b in range(z.nodes))
         mid = (mid + old[0] + STEP_HALF * stiff * old[1]) * inverse
         end = sum(quad_weights[1][b] * source[b] for b in range(z.nodes))
-        end = end + mid + STEP_HALF * stiff * old[2]
-        evals.append(old[1])
-        evals.append(mid)
-        later.append((end, inverse))
-        old_of.append(old)
-        mid_of.append(mid)
+        return old, mid, end + mid + STEP_HALF * stiff * old[2], inverse
+
+    evals = []
+    for w in range(z.n_wave):
+        part = modes[:, 2 * w * LANES : 2 * (w + 1) * LANES]
+        old, mid, _, _ = advance(part, table["stiff"].get(w * per_node, per_node))
+        evals += [old[1], mid]
 
     level_values = matmul_split(table["mix_from"].get(), jnp.concatenate(evals, 1))
     for w in range(z.n_wave):
@@ -693,35 +705,34 @@
         back = matmul(quad("coarse_quad", a, both_c), coarse_product_s[a])
         values = back * gauss
         for c in range(2):
-            at = (a * 2 + c) * z.slot_pitch
-            coarse_back_s[at : at + z.coarse_columns, :] = values[c * z.coarse_columns :][: z.coarse_columns]
-
-    tends = []
-    for w in range(z.n_wave):
-        left = jnp.concatenate(
-            [
-                coarse_back_s[pl.ds(w * slots + s, per_node, stride=z.slot_pitch), :].astype(bf)
-                for s in range(slots)
-            ],
-            0,
-        )
-        out = matmul(left, legendre_s[w, :, :LANES])
-        total = None
-        for s in range(slots):
-            term = slot(w, s) * out[s * per_node : (s + 1) * per_node]
-            total = term if total is None else total + term
-        tends.append(total)
-    coarse_modes = matmul_split(table["mix_back"].get(), jnp.concatenate(tends, 1))
-    for w in range(z.n_wave):
-        end, inverse = later[w]
-        end = (end + STEP_HALF * coarse_modes[:, w * LANES : (w + 1) * LANES]) * inverse
-        change_s[w, :per_node, :] = mid_of[w] - old_of[w][1]
-        change_s[w, per_node:, :] = end - old_of[w][2]
+            coarse_back_s[pl.ds(a * 2 + c, z.coarse_columns, stride=z.slot_pitch), :] = values[
+                c * z.coarse_columns : (c + 1) * z.coarse_columns
+            ]
 
     place = lax.axis_index("wave")
+    begin = place * (slots * z.slot_pitch)
+    left = jnp.concatenate(
+        [
+            coarse_back_s[pl.ds(pl.multiple_of(begin + s * z.slot_pitch, SUBLANES), per_node), :].astype(bf)
+            for s in range(slots)
+        ],
+        0,
+    )
+    out = matmul(left, legendre_s[place][:, :LANES])
+    wave_row = lax.broadcasted_iota(jnp.int32, (z.n_wave, LANES), 0)
+    total = None
+    for s in range(slots):
+        block = table["slot"].get(s * z.n_wave, z.n_wave)
+        mask = jnp.sum(jnp.where(wave_row == place, block, 0.0), axis=0, keepdims=True)
+        term = mask * out[s * per_node : (s + 1) * per_node]
+        total = term if total is None else total + term
+    coarse_modes = matmul_split(table["mix_back"].get(), total)
+    old, mid, end, inverse = advance(modes_s[place], table["stiff"].rows(place, per_node))
+    end = (end + STEP_HALF * coarse_modes) * inverse
+    change = jnp.concatenate([mid - old[1], end - old[2]], 0)
     begin = pl.multiple_of(lax.div(lax.axis_index("lev"), 2) * (2 * z.dev_rows), SUBLANES)
     mine = tend_s[place, pl.ds(begin, z.state_rows), :]
-    raised = matmul_split(table["lift"].get(), change_s[place])
+    raised = matmul_split(table["lift"].get(), change)
     lane = lax.broadcasted_iota(jnp.int32, (z.state_rows, wide), 1)
     for s in range(slots):
         low = mine if s == 0 else pltpu.roll(mine, wide - s * z.coarse, 1)
@@ -798,7 +809,6 @@
     bf, f32 = jnp.bfloat16, jnp.float32
     longitudes = grid_coef.shape[1]
     vmem = pl.BlockSpec(memory_space=pltpu.VMEM)
-    smem = pl.BlockSpec(memory_space=pltpu.SMEM)
     hbm = pl.BlockSpec(memory_space=pltpu.HBM)
     shape = jax.ShapeDtypeStruct
     stored = jnp.swapaxes(fine_state, 2, 3)
@@ -840,13 +850,13 @@
     basis = basis[:, : longitudes // 2]
     constants = [jnp.asarray(c, bf) for c in (basis, spread, sampled, coarse_sampled)]
     layout, picks = mix_constants(z)
-    staged = [fold_pairs[None], grid_coef, *constants, modes_from, modes_to, picks]
+    staged = [fold_pairs[None], mode_rates[None], grid_coef, *constants, modes_from, modes_to, picks]
     wide = 2 * LANES
     narrow_shape, full_shape, quads_shape = [entry[1] for entry in parts(z)]
     narrow, full, quads = pl.pallas_call(
         functools.partial(tables_kernel, z, layout),
         out_shape=(shape(narrow_shape, bf), shape(full_shape, f32), shape(quads_shape, bf)),
-        in_specs=[smem, smem] + [hbm] * len(staged),
+        in_specs=[hbm] * len(staged),
         out_specs=(vmem,) * 3,
         scratch_shapes=[
             pltpu.VMEM((2, z.own_levels * 2 * z.fine_width, longitudes // 2), bf),
@@ -855,7 +865,7 @@
         + [pltpu.VMEM(array.shape, array.dtype) for array in staged],
         cost_estimate=pl.CostEstimate(flops=10**9, bytes_accessed=4 * 10**6, transcendentals=0),
         name="tables",
-    )(mode_rates, fold_pairs, *staged)
+    )(*staged)
 
     partners = [(i, i ^ 1) for i in range(2 * z.chips)]
     other_quads = lax.ppermute(quads, ("wave", "lev"), partners)
@@ -878,8 +888,8 @@
             pltpu.VMEM((z.rows * z.column_pitch, lat_rows), f32),
             pltpu.VMEM((z.n_wave, z.rows + SUBLANES, wide), f32),
             pltpu.VMEM((z.mode_pitch * z.coarse_columns, lat_rows), f32),
-            pltpu.VMEM((z.per_node * z.slot_pitch, lat_rows), f32),
-            pltpu.VMEM((z.n_wave, (z.nodes - 1) * z.per_node, LANES), f32),
+            pltpu.VMEM((z.coarse_columns * z.slot_pitch, lat_rows), f32),
+            pltpu.VMEM((z.n_wave, z.rows, 2 * LANES), f32),
             pltpu.VMEM(narrow_shape, bf),
             pltpu.VMEM(full_shape, f32),
             pltpu.VMEM(quads_shape, bf),

time: 23.2 us -> 23.1 us (level)
  Pallas kernels: 10.7 us -> 10 us
  waiting for transfers between devices: 2.53 us -> 3.19 us
    pallas_call x1, Pallas kernels: 4.67 us -> 4.01 us  [replicated_plan(): pl.pallas_call(functools.partial(tables_kernel, z, layout), out_shape=(sh...]
    ppermute x1, waiting for transfers between devices: 0.69 us -> 0.03 us  [replicated_plan(): other_quads = lax.ppermute(quads, ('wave', 'lev'), partners)]
    all_to_all x1, waiting for transfers between devices: 1.09 us -> 1.75 us  [replicated_plan(): lax.all_to_all(block, ('wave', 'lev'), 0, 0, tiled=True, axis_index_group...]
    ppermute x1, waiting for transfers between devices: 0.75 us -> 1.41 us  [replicated_plan(): other = lax.ppermute(own, ('wave', 'lev'), partners)]
  transfers between devices with their start and end apart: 3 -> 3, of which waited for: 3 -> 2; matrix products, arithmetic and copies ran while one was open for 0% -> 0% of each run, Pallas kernels for 20% -> 18%
where the time goes in v5:
time: 23.1 us; the launch traced here: 22.8 us
  Pallas kernels  10 us (43%)
  starting transfers between devices  8.9 us (39%)
  waiting for transfers between devices  3.19 us (14%)
  between operations  0.66 us (3%)
    all_to_all x1, starting transfers between devices, replicated_plan(): lax.all_to_all(block, ('wave', 'lev'), 0, 0, tiled=True, axis_index_group...  8.82 us
    pallas_call x1, Pallas kernels, replicated_plan(): pl.pallas_call(functools.partial(sweep_kernel, z), out_shape=(shape((z.le...  4.37 us
    pallas_call x1, Pallas kernels, replicated_plan(): pl.pallas_call(functools.partial(tables_kernel, z, layout), out_shape=(sh...  4.01 us
    all_to_all x1, waiting for transfers between devices, replicated_plan(): lax.all_to_all(block, ('wave', 'lev'), 0, 0, tiled=True, axis_index_group...  1.75 us
    pallas_call x1, Pallas kernels, replicated_plan(): pl.pallas_call(functools.partial(pack_kernel, z), out_shape=shape((z.chip...  1.63 us
    ppermute x1, waiting for transfers between devices, replicated_plan(): other = lax.ppermute(own, ('wave', 'lev'), partners)  1.41 us
  transfers between devices with their start and end apart: 3, of which 2 were waited for; matrix products, arithmetic and copies ran while one was open for 0% of the time, Pallas kernels for 18%

profile of v5, /device:TPU:0, one launch (start us, length us, event | category | flops | bytes accessed | tf_op | source)
XLA Modules:
  0.0 22.8 jit_solution(10820946909532786261)
XLA Ops:
  0.6 1.6 %pack.1 = bf16[16,48,128]{2,1,0:T(8,128)(2,1)} custom-call(f32[2,3,3,2,49]{4,3,2,1,0:T(2,128)} %bitcast.6, bf16[3,24,49]{2,1,0:T(8,128)(2,1)} %leg_hbm.1, f32[1,24]{1,0:T(1,128)} %bitcast.8), custom_call_target="tpu_custom_call" | custom-call | tf_op jit(solution)/shard_map/pack/pallas_call | solution.py:815
  2.3 8.8 %all-to-all-start = ((bf16[16,48,128]{2,1,0:T(8,128)(2,1)}), bf16[16,48,128]{2,1,0:T(8,128)(2,1)S(1)}, u32[]{:S(2)}, u32[]{:S(2)}) async-start(bf16[16,48,128]{2,1,0:T(8,128)(2,1)} %pack.1), calls=%async_computation | async-start | bytes 393216 | tf_op jit(solution)/shard_map/all_to_all | solution.py:830
  11.1 0.0 copy-start
  11.1 4.0 %tables.1 = (bf16[384,144]{1,0:T(8,128)(2,1)}, f32[224,256]{1,0:T(8,128)}, bf16[576,192]{1,0:T(8,128)(2,1)}) custom-call(s32[1,24]{1,0:T(1,128)} %bitcast.11, f32[1,8]{1,0:T(1,128)} %bitcast.12, f32[8,2560]{1,0:T(8,128)} %refs_2_.1, bf16[96,1280]{1,0:T(8,128)(2,1)} %constant.10.clone.refs_3_, bf16[2,1280,144]{2,1,0:T(8,128)(2,1)} %constant.11.clone.refs_4_, ...), custom_call_target="tpu_custom_call" | custom-call | flops 1000000000 | bytes 4000000 | tf_op jit(solution)/shard_map/tables/pallas_call | solution.py:856
  15.1 0.1 collective-permute-start.1
  15.2 1.8 %all-to-all-done.own_ref = bf16[16,48,128]{2,1,0:T(8,128)(2,1)S(1)} async-done(((bf16[16,48,128]{2,1,0:T(8,128)(2,1)}), bf16[16,48,128]{2,1,0:T(8,128)(2,1)S(1)}, u32[]{:S(2)}, u32[]{:S(2)}) %all-to-all-start) | async-done | bytes 196640 | tf_op jit(solution)/shard_map/all_to_all | solution.py:830
  16.9 0.0 collective-permute-start
  16.9 0.0 collective-permute-done.1.other_quads_hbm
  17.0 0.0 copy-start.1
  17.0 1.4 %collective-permute-done.other_ref = bf16[16,48,128]{2,1,0:T(8,128)(2,1)S(1)} collective-permute-done((bf16[16,48,128]{2,1,0:T(8,128)(2,1)S(1)}, bf16[16,48,128]{2,1,0:T(8,128)(2,1)S(1)}, u32[]{:S(2)}, u32[]{:S(2)}) %collective-permute-start) | collective-permute-done | bytes 196640 | tf_op jit(solution)/shard_map/ppermute | solution.py:873
  18.4 0.0 copy-done.1
  18.4 0.0 copy-done
  18.4 4.4 %sweep.1 = (f32[2,2,3,2,49]{4,3,2,1,0:T(2,128)}, f32[2,3,3,2,49]{4,3,2,1,0:T(2,128)}) custom-call(bf16[16,48,128]{2,1,0:T(8,128)(2,1)S(1)} %all-to-all-done.own_ref, bf16[16,48,128]{2,1,0:T(8,128)(2,1)S(1)} %collective-permute-done.other_ref, f32[2,3,3,2,49]{4,3,2,1,0:T(2,128)S(1)} %bitcast.7, bf16[384,144]{1,0:T(8,128)(2,1)} %get-tuple-element.11.narrow_hbm, ...), custom_call_target="tpu_custom_call" | custom-call | tf_op jit(solution)/shard_map/sweep/pallas_call | solution.py:876
Async XLA Ops:
  2.3 14.7 %all-to-all-start = ((bf16[16,48,128]{2,1,0:T(8,128)(2,1)}), bf16[16,48,128]{2,1,0:T(8,128)(2,1)S(1)}, u32[]{:S(2)}, u32[]{:S(2)}) async-start(bf16[16,48,128]{2,1,0:T(8,128)(2,1)} %pack.1), calls=%async_computation | async-start | bytes 393216 | tf_op jit(solution)/shard_map/all_to_all | solution.py:830
  11.1 7.3 %copy-start = (f32[2,3,2,3,49]{4,2,3,1,0:T(2,128)S(1)}, f32[2,3,2,3,49]{4,2,3,1,0:T(2,128)}, u32[]{:S(2)}) copy-start(f32[2,3,2,3,49]{4,2,3,1,0:T(2,128)} %param.13) | copy-start | bytes 21172
  15.1 1.9 %collective-permute-start.1 = (bf16[576,192]{1,0:T(8,128)(2,1)}, bf16[576,192]{1,0:T(8,128)(2,1)S(1)}, u32[]{:S(2)}, u32[]{:S(2)}) collective-permute-start(bf16[576,192]{1,0:T(8,128)(2,1)} %get-tuple-element.13.quads_hbm), channel_id=1, source_target_pairs={{0,1},{1,0},{2,3},{3,2},{4,5},{5,4},{6,7},{7,6},{8,9},{9,8},{10,11... | collective-permute-start | bytes 663560 | tf_op jit(solution)/shard_map/ppermute | solution.py:871
  16.9 1.4 %collective-permute-start = (bf16[16,48,128]{2,1,0:T(8,128)(2,1)S(1)}, bf16[16,48,128]{2,1,0:T(8,128)(2,1)S(1)}, u32[]{:S(2)}, u32[]{:S(2)}) collective-permute-start(bf16[16,48,128]{2,1,0:T(8,128)(2,1)S(1)} %all-to-all-done.own_ref), channel_id=1, source_target_pairs={{0,1},{1,0},{2,3},{3,2},{4,5},{5,4},{6,7},{7,6},{8,9},{9,8},{10,11... | collective-permute-start | bytes 589832 | tf_op jit(solution)/shard_map/ppermute | solution.py:873
  17.0 1.4 %copy-start.1 = (bf16[576,192]{1,0:T(8,128)(2,1)}, bf16[576,192]{1,0:T(8,128)(2,1)S(1)}, u32[]{:S(2)}) copy-start(bf16[576,192]{1,0:T(8,128)(2,1)S(1)} %collective-permute-done.1.other_quads_hbm) | copy-start | bytes 663556

commit v6 on v5

--- a/solution.py
+++ b/solution.py
@@ -884,11 +884,11 @@
         scratch_shapes=[
             pltpu.VMEM((z.n_wave, lat_rows, wide), f32),
             pltpu.VMEM((z.n_wave, z.rows, wide), f32),
-            pltpu.VMEM((z.row_pitch * z.fine_columns, lat_rows), f32),
-            pltpu.VMEM((z.rows * z.column_pitch, lat_rows), f32),
+            pltpu.VMEM((z.row_pitch * (z.fine_columns + 1), lat_rows), f32),
+            pltpu.VMEM(((z.rows + 1) * z.column_pitch, lat_rows), f32),
             pltpu.VMEM((z.n_wave, z.rows + SUBLANES, wide), f32),
-            pltpu.VMEM((z.mode_pitch * z.coarse_columns, lat_rows), f32),
-            pltpu.VMEM((z.coarse_columns * z.slot_pitch, lat_rows), f32),
+            pltpu.VMEM((z.mode_pitch * (z.coarse_columns + 1), lat_rows), f32),
+            pltpu.VMEM(((z.coarse_columns + 1) * z.slot_pitch, lat_rows), f32),
             pltpu.VMEM((z.n_wave, z.rows, 2 * LANES), f32),
             pltpu.VMEM(narrow_shape, bf),
             pltpu.VMEM(full_shape, f32),

time: 23.1 us -> 23.1 us (level)
  no operation moved by 1% of the time
where the time goes in v6:
time: 23.1 us; the launch traced here: 22.8 us
  Pallas kernels  10 us (43%)
  starting transfers between devices  8.9 us (39%)
  waiting for transfers between devices  3.19 us (14%)
  between operations  0.66 us (3%)
    all_to_all x1, starting transfers between devices, replicated_plan(): lax.all_to_all(block, ('wave', 'lev'), 0, 0, tiled=True, axis_index_group...  8.82 us
    pallas_call x1, Pallas kernels, replicated_plan(): pl.pallas_call(functools.partial(sweep_kernel, z), out_shape=(shape((z.le...  4.36 us
    pallas_call x1, Pallas kernels, replicated_plan(): pl.pallas_call(functools.partial(tables_kernel, z, layout), out_shape=(sh...  4.01 us
    all_to_all x1, waiting for transfers between devices, replicated_plan(): lax.all_to_all(block, ('wave', 'lev'), 0, 0, tiled=True, axis_index_group...  1.75 us
    pallas_call x1, Pallas kernels, replicated_plan(): pl.pallas_call(functools.partial(pack_kernel, z), out_shape=shape((z.chip...  1.63 us
    ppermute x1, waiting for transfers between devices, replicated_plan(): other = lax.ppermute(own, ('wave', 'lev'), partners)  1.41 us
  transfers between devices with their start and end apart: 3, of which 2 were waited for; matrix products, arithmetic and copies ran while one was open for 0% of the time, Pallas kernels for 18%

profile of v6, /device:TPU:0, one launch (start us, length us, event | category | flops | bytes accessed | tf_op | source)
XLA Modules:
  0.0 22.8 jit_solution(3453996322320482895)
XLA Ops:
  0.6 1.6 %pack.1 = bf16[16,48,128]{2,1,0:T(8,128)(2,1)} custom-call(f32[2,3,3,2,49]{4,3,2,1,0:T(2,128)} %bitcast.6, bf16[3,24,49]{2,1,0:T(8,128)(2,1)} %leg_hbm.1, f32[1,24]{1,0:T(1,128)} %bitcast.8), custom_call_target="tpu_custom_call" | custom-call | tf_op jit(solution)/shard_map/pack/pallas_call | solution.py:815
  2.3 8.8 %all-to-all-start = ((bf16[16,48,128]{2,1,0:T(8,128)(2,1)}), bf16[16,48,128]{2,1,0:T(8,128)(2,1)S(1)}, u32[]{:S(2)}, u32[]{:S(2)}) async-start(bf16[16,48,128]{2,1,0:T(8,128)(2,1)} %pack.1), calls=%async_computation | async-start | bytes 393216 | tf_op jit(solution)/shard_map/all_to_all | solution.py:830
  11.1 0.0 copy-start
  11.1 4.0 %tables.1 = (bf16[384,144]{1,0:T(8,128)(2,1)}, f32[224,256]{1,0:T(8,128)}, bf16[576,192]{1,0:T(8,128)(2,1)}) custom-call(s32[1,24]{1,0:T(1,128)} %bitcast.11, f32[1,8]{1,0:T(1,128)} %bitcast.12, f32[8,2560]{1,0:T(8,128)} %refs_2_.1, bf16[96,1280]{1,0:T(8,128)(2,1)} %constant.10.clone.refs_3_, bf16[2,1280,144]{2,1,0:T(8,128)(2,1)} %constant.11.clone.refs_4_, ...), custom_call_target="tpu_custom_call" | custom-call | flops 1000000000 | bytes 4000000 | tf_op jit(solution)/shard_map/tables/pallas_call | solution.py:856
  15.1 0.1 collective-permute-start.1
  15.2 1.8 %all-to-all-done.own_ref = bf16[16,48,128]{2,1,0:T(8,128)(2,1)S(1)} async-done(((bf16[16,48,128]{2,1,0:T(8,128)(2,1)}), bf16[16,48,128]{2,1,0:T(8,128)(2,1)S(1)}, u32[]{:S(2)}, u32[]{:S(2)}) %all-to-all-start) | async-done | bytes 196640 | tf_op jit(solution)/shard_map/all_to_all | solution.py:830
  16.9 0.0 collective-permute-start
  16.9 0.0 collective-permute-done.1.other_quads_hbm
  17.0 0.0 copy-start.1
  17.0 1.4 %collective-permute-done.other_ref = bf16[16,48,128]{2,1,0:T(8,128)(2,1)S(1)} collective-permute-done((bf16[16,48,128]{2,1,0:T(8,128)(2,1)S(1)}, bf16[16,48,128]{2,1,0:T(8,128)(2,1)S(1)}, u32[]{:S(2)}, u32[]{:S(2)}) %collective-permute-start) | collective-permute-done | bytes 196640 | tf_op jit(solution)/shard_map/ppermute | solution.py:873
  18.4 0.0 copy-done.1
  18.4 0.0 copy-done
  18.4 4.4 %sweep.1 = (f32[2,2,3,2,49]{4,3,2,1,0:T(2,128)}, f32[2,3,3,2,49]{4,3,2,1,0:T(2,128)}) custom-call(bf16[16,48,128]{2,1,0:T(8,128)(2,1)S(1)} %all-to-all-done.own_ref, bf16[16,48,128]{2,1,0:T(8,128)(2,1)S(1)} %collective-permute-done.other_ref, f32[2,3,3,2,49]{4,3,2,1,0:T(2,128)S(1)} %bitcast.7, bf16[384,144]{1,0:T(8,128)(2,1)} %get-tuple-element.11.narrow_hbm, ...), custom_call_target="tpu_custom_call" | custom-call | tf_op jit(solution)/shard_map/sweep/pallas_call | solution.py:876
Async XLA Ops:
  2.3 14.7 %all-to-all-start = ((bf16[16,48,128]{2,1,0:T(8,128)(2,1)}), bf16[16,48,128]{2,1,0:T(8,128)(2,1)S(1)}, u32[]{:S(2)}, u32[]{:S(2)}) async-start(bf16[16,48,128]{2,1,0:T(8,128)(2,1)} %pack.1), calls=%async_computation | async-start | bytes 393216 | tf_op jit(solution)/shard_map/all_to_all | solution.py:830
  11.1 7.3 %copy-start = (f32[2,3,2,3,49]{4,2,3,1,0:T(2,128)S(1)}, f32[2,3,2,3,49]{4,2,3,1,0:T(2,128)}, u32[]{:S(2)}) copy-start(f32[2,3,2,3,49]{4,2,3,1,0:T(2,128)} %param.13) | copy-start | bytes 21172
  15.1 1.9 %collective-permute-start.1 = (bf16[576,192]{1,0:T(8,128)(2,1)}, bf16[576,192]{1,0:T(8,128)(2,1)S(1)}, u32[]{:S(2)}, u32[]{:S(2)}) collective-permute-start(bf16[576,192]{1,0:T(8,128)(2,1)} %get-tuple-element.13.quads_hbm), channel_id=1, source_target_pairs={{0,1},{1,0},{2,3},{3,2},{4,5},{5,4},{6,7},{7,6},{8,9},{9,8},{10,11... | collective-permute-start | bytes 663560 | tf_op jit(solution)/shard_map/ppermute | solution.py:871
  16.9 1.4 %collective-permute-start = (bf16[16,48,128]{2,1,0:T(8,128)(2,1)S(1)}, bf16[16,48,128]{2,1,0:T(8,128)(2,1)S(1)}, u32[]{:S(2)}, u32[]{:S(2)}) collective-permute-start(bf16[16,48,128]{2,1,0:T(8,128)(2,1)S(1)} %all-to-all-done.own_ref), channel_id=1, source_target_pairs={{0,1},{1,0},{2,3},{3,2},{4,5},{5,4},{6,7},{7,6},{8,9},{9,8},{10,11... | collective-permute-start | bytes 589832 | tf_op jit(solution)/shard_map/ppermute | solution.py:873
  17.0 1.4 %copy-start.1 = (bf16[576,192]{1,0:T(8,128)(2,1)}, bf16[576,192]{1,0:T(8,128)(2,1)S(1)}, u32[]{:S(2)}) copy-start(bf16[576,192]{1,0:T(8,128)(2,1)S(1)} %collective-permute-done.1.other_quads_hbm) | copy-start | bytes 663556
